TPU v7x, 128 devices: a whole 4x4x4 slice. The times are simulated.
128 devices in a mesh: lat: 16 (over y, z), lon: 8 (over x, core).
Axes of the slice: x: 4, y: 4, z: 4, core: 2. Of those that a mesh axis runs over, the one named last changes fastest.
Arguments:
- inputs: bfloat16 [640, 1440, 256], P('lat', 'lon'), may hold values from -6 to 6
- w_enc: bfloat16 [3, 3, 256, 256], replicated, may hold values from -0.125 to 0.125
- w_proj: bfloat16 [256, 128], replicated, may hold values from -0.375 to 0.375
- film_scale: float32 [720, 128], replicated, may hold values from -3 to 3
- film_shift: float32 [720, 128], replicated, may hold values from -3 to 3
- lead_ids: int32 [16], replicated, may hold values from 0 to 719
- w_head: bfloat16 [3, 3, 128, 128], replicated, may hold values from -0.1875 to 0.1875
- zonal_mix: bfloat16 [720, 720], replicated, may hold values from -0.21875 to 0.21875
Outputs:
- forecast: bfloat16 [16, 320, 720, 128], P('lon', 'lat')
Inputs may be any that keep to these rules, and one draw needn't show every extreme that they name: `lead_ids`: rows of the tables; repeats may occur.
All inputs are finite; a program needn't handle non-finite values.
Results may differ from a plain program's by a relative error of at most 0.015.
Values may be sent and summed in bfloat16 or wider, within the bound.
A program may use at most 128 MiB of HBM per device.

v0:
```python
import jax
import jax.numpy as jnp
from jax import lax
from jax.sharding import PartitionSpec as P

LEAD_DEV = 2


def extended(x, sides, width, wrap):
    for axis, dim in sides:
        devices, length = (lax.axis_size(axis), x.shape[dim])
        up = [(i, (i + 1) % devices) for i in range(devices if wrap else devices - 1)]
        down = [(j, i) for i, j in up]
        last = lax.slice_in_dim(x, length - width, length, axis=dim)
        initial = lax.slice_in_dim(x, 0, width, axis=dim)
        before = lax.ppermute(last, axis, up)
        after = lax.ppermute(initial, axis, down)
        x = jnp.concatenate([before, x, after], axis=dim)
    return x


def conv_three(padded, weight):
    batched = padded if padded.ndim == 4 else padded[None]
    result = lax.conv_general_dilated(
        batched,
        weight,
        (1, 1),
        "VALID",
        dimension_numbers=("NHWC", "HWIO", "NHWC"),
        preferred_element_type=jnp.float32,
    )
    return result if padded.ndim == 4 else result[0]


def pool_pairs(field):
    summed = lax.reduce_window(
        field, jnp.array(0, field.dtype), lax.add, (2, 2, 1), (2, 2, 1), "VALID"
    )
    return summed * 0.25


def wrap_columns(field):
    return jnp.concatenate([field[..., -1:, :], field, field[..., :1, :]], axis=-2)


def modulate(projected, scales, shifts):
    widened = projected.astype(jnp.float32)[None]
    return (widened * (1.0 + scales[:, None, None, :]) + shifts[:, None, None, :]).astype(
        jnp.bfloat16
    )


def shards(inputs, w_enc, w_proj, film_scale, film_shift, lead_ids, w_head, zonal_mix):
    lat_rows, lon_cols, channels = inputs.shape
    with_rows = extended(inputs, (("lat", 0),), 1, False)
    padded = extended(with_rows, (("lon", 1),), 1, True)
    encoded = jax.nn.gelu(conv_three(padded, w_enc))
    pooled = pool_pairs(encoded).astype(jnp.bfloat16)
    head_width = w_proj.shape[1]
    lon_group = lax.axis_index("lon")
    my_rows = lax.dynamic_slice_in_dim(lead_ids, lon_group * LEAD_DEV, LEAD_DEV)
    flat = jnp.dot(pooled.reshape(-1, channels), w_proj, preferred_element_type=jnp.float32)
    band_proj = lax.all_gather(
        flat.astype(jnp.bfloat16).reshape(pooled.shape[0], pooled.shape[1], head_width),
        "lon",
        axis=1,
        tiled=True,
    )
    onehot = (my_rows[:, None] == jnp.arange(film_scale.shape[0], dtype=jnp.int32)[None, :]).astype(
        jnp.float32
    )
    scales = jnp.dot(onehot, film_scale, precision=lax.Precision.HIGHEST)
    shifts = jnp.dot(onehot, film_shift, precision=lax.Precision.HIGHEST)
    scales, shifts = (scales, shifts)
    with_band = None
    modulated = modulate(band_proj, scales, shifts)
    with_band = extended(modulated, (("lat", 1),), 1, False)
    padded_head = wrap_columns(with_band)
    hidden = jax.nn.gelu(conv_three(padded_head, w_head)).astype(jnp.bfloat16)
    mixed = jnp.einsum("ij,bajc->baic", zonal_mix, hidden, preferred_element_type=jnp.float32)
    return (modulated.astype(jnp.float32) + mixed).astype(jnp.bfloat16)


def solution(mesh):
    in_specs = (P("lat", "lon", None), P(), P(), P(), P(), P(), P(), P())
    out_specs = P("lon", "lat", None, None)
    return jax.shard_map(shards, mesh=mesh, in_specs=in_specs, out_specs=out_specs, check_vma=False)
```

profile of v0, /device:TPU:24, one launch (start us, length us, event | category | flops | bytes accessed | tf_op | source)
XLA Modules:
  0.0 218.8 jit_solution(3243540371353144879)
XLA Ops:
  6.5 1.8 fusion.43
  8.4 6.3 %collective-permute-start.1 = (bf16[1,180,256]{2,1,0:T(8,128)(2,1)S(1)}, bf16[1,180,256]{2,1,0:T(8,128)(2,1)S(1)}, u32[]{:S(2)}, u32[]{:S(2)}) collective-permute-start(bf16[1,180,256]{2,1,0:T(8,128)(2,1)S(1)} %copy.64), channel_id=1, source_target_pairs={{8,0},{16,8},{24,16},{32,24},{40,32},{48,40},{56,48},{64,56},{72,6... | collective-permute-start | bytes 276488 | tf_op jit(solution)/shard_map/ppermute | solution.py:17
  14.6 1.9 collective-permute-start
  16.6 0.2 collective-permute-done.1
  16.8 0.1 copy.46
  16.9 6.3 %collective-permute-done = bf16[1,180,256]{2,1,0:T(8,128)(2,1)S(1)} collective-permute-done((bf16[1,180,256]{2,1,0:T(8,128)(2,1)S(1)}, bf16[1,180,256]{2,1,0:T(8,128)(2,1)S(1)}, u32[]{:S(2)}, u32[]{:S(2)}) %collective-permute-start) | collective-permute-done | bytes 92192 | tf_op jit(solution)/shard_map/ppermute | solution.py:16
  23.2 0.1 copy.45
  23.4 0.8 pad_maximum_fusion.6
  24.1 0.0 collective-permute-start.2
  24.2 2.9 %collective-permute-start.3 = (bf16[42,1,256]{2,0,1:T(8,128)(2,1)S(1)}, bf16[42,1,256]{2,0,1:T(8,128)(2,1)S(1)}, u32[]{:S(2)}, u32[]{:S(2)}) collective-permute-start(bf16[42,1,256]{2,0,1:T(8,128)(2,1)S(1)} %get-tuple-element.8), channel_id=1, source_target_pairs={{1,0},{2,1},{3,2},{4,3},{5,4},{6,5},{7,6},{0,7},{9,8},{10,9},{11,1... | collective-permute-start | bytes 64520 | tf_op jit(solution)/shard_map/ppermute | solution.py:17
  27.1 1.5 collective-permute-done.2
  28.6 0.0 collective-permute-done.3
  28.6 3.2 %maximum_bitcast_fusion = bf16[42,1,182,256]{3,0,2,1:T(8,128)(2,1)S(1)} fusion(bf16[42,1,256]{2,0,1:T(8,128)(2,1)S(1)} %collective-permute-done.3, bf16[1,180,256]{2,0,1:T(2,128)(2,1)S(1)} %copy.46, bf16[40,180,256]{2,0,1:T(8,128)(2,1)S(1)} %copy-done.2, bf16[1,180,256]{2,0,1:T(2,128)(2,1)S(1)} %copy.45, bf16[42,1,256]{2,0,1:T(8,128)(2,1)S(1)} %collective-permute-done.2), kind=kLoop, calls=%fused_computation.37 | loop fusion | flops 19568640 | bytes 7827456 | tf_op jit(solution)/shard_map/broadcast_in_dim | solution.py:23
  31.8 0.4 pad
  32.2 1.5 copy.49
  33.7 0.1 slice.36
  33.8 9.5 %broadcast_select_fusion = f32[40,8,23,256]{3,1,2,0:T(8,128)S(1)} fusion(pred[8,23]{0,1:T(8,128)(4,1)S(1)} %copy-done.9, bf16[3,3,256,256]{3,2,1,0:T(8,128)(2,1)S(1)} %copy-done, bf16[42,1,7,2,256]{4,2,3,0,1:T(8,128)(2,1)S(1)} %slice.36, bf16[42,1,8,23,256]{4,2,3,0,1:T(8,128)(2,1)S(1)} %copy.49), kind=kOutput, calls=%fused_computation.44 | convolution fusion | flops 8696995840 | bytes 12974264 | tf_op jit(solution)/shard_map/conv_general_dilated | solution.py:24
  43.3 2.6 %copy.50 = f32[40,8,23,256]{3,0,2,1:T(8,128)S(1)} copy(f32[40,8,23,256]{3,1,2,0:T(8,128)S(1)} %broadcast_select_fusion) | data formatting | bytes 15073280 | tf_op jit(solution)/shard_map/conv_general_dilated | solution.py:24
  45.9 4.2 %fusion.23 = f32[40,180,256]{2,0,1:T(8,128)} fusion(f32[40,1,184,256]{3,0,2,1:T(8,128)S(1)} %bitcast.42), kind=kLoop, calls=%fused_computation.33 | loop fusion | flops 14745600 | bytes 14745600 | tf_op jit(solution)/shard_map/mul | solution.py:57
  50.1 8.4 %reduce_window.7 = f32[20,90,256]{2,0,1:T(8,128)S(1)} reduce-window(f32[40,180,256]{2,0,1:T(8,128)} %fusion.23, f32[]{:T(128)} %constant.14.clone.1), window={size=2x2x1 stride=2x2x1}, to_apply=%region_0.0 | reduce-window | flops 1382400 | bytes 9216004 | tf_op jit(solution)/shard_map/reduce_window | solution.py:36
  58.5 0.2 multiply_convert_fusion
  58.7 0.2 copy.51
  58.9 0.2 convert_element_type.27
  59.2 0.4 convolution_convert_fusion
  59.6 0.1 reshape.13
  59.7 1.0 copy.52
  60.7 0.0 all-gather.2.cloned.1.call-update
  60.8 0.1 dynamic_slice.3
  60.8 1.2 convolution_add_fusion
  62.1 0.3 fusion.36
  62.4 30.0 %all-gather.2.cloned.1.call-done = bf16[20,720,128]{2,0,1:T(8,128)(2,1)} async-done(((bf16[20,90,128]{2,0,1:T(8,128)(2,1)}), bf16[20,720,128]{2,0,1:T(8,128)(2,1)}) %all-gather.2.cloned.1.call-update) | async-done | bytes 3686416 | tf_op jit(solution)/shard_map/all_gather | solution.py:63
  92.4 5.8 %copy_convert_fusion = f32[20,720,128]{2,1,0:T(8,128)} fusion(bf16[20,720,128]{2,0,1:T(8,128)(2,1)} %all-gather.2.cloned.1.call-done), kind=kLoop, calls=%fused_computation.45 | loop fusion | flops 1843200 | bytes 11059200 | tf_op jit(solution)/shard_map/convert_element_type | solution.py:47
  98.2 7.6 %add_convert_fusion = bf16[2,20,720,128]{3,2,1,0:T(8,128)(2,1)} fusion(f32[2,128]{1,0:T(2,128)S(1)} %fusion.36, f32[2,128]{1,0:T(2,128)S(1)} %convolution_add_fusion, f32[20,720,128]{2,1,0:T(8,128)} %copy_convert_fusion), kind=kLoop, calls=%fused_computation.13 | loop fusion | flops 11059200 | bytes 14747648 | tf_op jit(solution)/shard_map/convert_element_type | solution.py:48
  105.8 1.1 fusion.42
  107.0 3.5 %collective-permute-start.4 = (bf16[2,1,720,128]{3,2,1,0:T(8,128)(2,1)S(1)}, bf16[2,1,720,128]{3,2,1,0:T(8,128)(2,1)S(1)}, u32[]{:S(2)}, u32[]{:S(2)}) collective-permute-start(bf16[2,1,720,128]{3,2,1,0:T(8,128)(2,1)S(1)} %get-tuple-element.5), channel_id=1, source_target_pairs={{0,8},{8,16},{16,24},{24,32},{32,40},{40,48},{48,56},{56,64},{64,7... | collective-permute-start | bytes 1105928 | tf_op jit(solution)/shard_map/ppermute | solution.py:16
  110.4 4.5 %collective-permute-start.5 = (bf16[2,1,720,128]{3,2,1,0:T(8,128)(2,1)S(1)}, bf16[2,1,720,128]{3,2,1,0:T(8,128)(2,1)S(1)}, u32[]{:S(2)}, u32[]{:S(2)}) collective-permute-start(bf16[2,1,720,128]{3,2,1,0:T(8,128)(2,1)S(1)} %get-tuple-element.6), channel_id=1, source_target_pairs={{8,0},{16,8},{24,16},{32,24},{40,32},{48,40},{56,48},{64,56},{72,6... | collective-permute-start | bytes 1105928 | tf_op jit(solution)/shard_map/ppermute | solution.py:17
  114.9 6.8 %collective-permute-done.4 = bf16[2,1,720,128]{3,2,1,0:T(8,128)(2,1)S(1)} collective-permute-done((bf16[2,1,720,128]{3,2,1,0:T(8,128)(2,1)S(1)}, bf16[2,1,720,128]{3,2,1,0:T(8,128)(2,1)S(1)}, u32[]{:S(2)}, u32[]{:S(2)}) %collective-permute-start.4) | collective-permute-done | bytes 368672 | tf_op jit(solution)/shard_map/ppermute | solution.py:16
  121.7 1.2 collective-permute-done.5
  122.9 13.0 %fusion.15 = bf16[22,2,722,128]{3,2,0,1:T(8,128)(2,1)} fusion(bf16[2,1,720,128]{3,2,1,0:T(8,128)(2,1)S(1)} %collective-permute-done.5, bf16[2,20,720,128]{3,2,1,0:T(8,128)(2,1)} %add_convert_fusion, bf16[2,1,720,128]{3,2,1,0:T(8,128)(2,1)S(1)} %collective-permute-done.4), kind=kLoop, calls=%fused_computation.22 | loop fusion | flops 73193472 | bytes 16242688 | tf_op jit(solution)/shard_map/concatenate | solution.py:43
  135.9 7.0 %pad.2 = bf16[22,2,728,128]{3,2,0,1:T(8,128)(2,1)} pad(bf16[22,2,722,128]{3,2,0,1:T(8,128)(2,1)} %fusion.15, bf16[]{:T(256)} %constant.6), padding=0_0x0_0x0_6x0_0 | pad | bytes 16332802 | tf_op jit(solution)/shard_map/concatenate | solution.py:43
  142.9 12.6 %reshape.39 = bf16[22,2,8,91,128]{4,3,2,0,1:T(8,128)(2,1)} reshape(bf16[22,2,728,128]{3,2,0,1:T(8,128)(2,1)} %pad.2) | data formatting | bytes 16400384 | tf_op jit(solution)/shard_map/conv_general_dilated | solution.py:24
  155.5 1.2 slice.40
  156.7 0.1 copy.77
  156.8 4.6 %fusion.10 = bf16[22,2,8,93,128]{4,3,2,1,0:T(8,128)(2,1)S(1)} fusion(bf16[22,2,7,2,128]{4,3,2,1,0:T(2,128)(2,1)S(1)} %copy.77, bf16[22,2,8,91,128]{4,3,2,0,1:T(8,128)(2,1)} %reshape.39), kind=kLoop, calls=%fused_computation.15 | loop fusion | flops 25141248 | bytes 16738304 | tf_op jit(solution)/shard_map/conv_general_dilated | solution.py:24
  161.5 21.3 %fusion.8 = bf16[20,16,91,128]{3,1,2,0:T(8,128)(2,1)S(1)} fusion(bf16[3,3,128,128]{3,2,1,0:T(8,128)(2,1)S(1)} %copy-done.6, bf16[22,2,8,93,128]{4,3,2,1,0:T(8,128)(2,1)S(1)} %fusion.10, pred[16,91]{0,1:T(8,128)(4,1)S(1)} %copy-done.8), kind=kOutput, calls=%fused_computation.10 | convolution fusion | flops 8625111040 | bytes 16131504 | tf_op jit(solution)/shard_map/conv_general_dilated | solution.py:24
  182.8 5.1 %copy.56 = bf16[20,16,91,128]{3,2,1,0:T(8,128)(2,1)} copy(bf16[20,16,91,128]{3,1,2,0:T(8,128)(2,1)S(1)} %fusion.8) | data formatting | bytes 14909440 | tf_op jit(solution)/shard_map/convert_element_type | solution.py:79
  187.9 11.6 %reshape.27 = bf16[20,2,728,128]{3,2,1,0:T(8,128)(2,1)} reshape(bf16[20,16,91,128]{3,2,1,0:T(8,128)(2,1)} %copy.56) | data formatting | bytes 14909440 | tf_op jit(solution)/shard_map/convert_element_type | solution.py:79
  199.4 12.3 %fusion.9 = bf16[2,20,720,128]{3,2,1,0:T(8,128)(2,1)} fusion(bf16[2,20,720,128]{3,2,1,0:T(8,128)(2,1)} %add_convert_fusion, bf16[720,720]{1,0:T(8,128)(2,1)S(1)} %copy-done.5, bf16[20,2,728,128]{3,2,1,0:T(8,128)(2,1)} %reshape.27), kind=kOutput, calls=%fused_computation.12 | convolution fusion | flops 5319475200 | bytes 23155200 | tf_op jit(solution)/shard_map/ij,bajc->baic/dot_general | solution.py:80
  (23 shorter events, 0.1 us)
Async XLA Ops:
  6.5 27.3 %copy-start = (bf16[3,3,256,256]{3,2,1,0:T(8,128)(2,1)S(1)}, bf16[3,3,256,256]{3,2,1,0:T(8,128)(2,1)}, u32[]{:S(2)}) copy-start(bf16[3,3,256,256]{3,2,1,0:T(8,128)(2,1)} %param.9) | copy-start | bytes 3538948
  6.5 85.8 %all-gather.2.cloned.1.call-start = ((), (), s32[]{:S(2)}) async-start(), calls=%async_computation | async-start | bytes 4976640 | tf_op jit(solution)/shard_map/all_gather | solution.py:63
  6.5 22.1 %copy-start.2 = (bf16[40,180,256]{2,0,1:T(8,128)(2,1)S(1)}, bf16[40,180,256]{2,0,1:T(8,128)(2,1)}, u32[]{:S(2)}) copy-start(bf16[40,180,256]{2,0,1:T(8,128)(2,1)} %param.8) | copy-start | bytes 11059204
  8.4 8.4 %collective-permute-start.1 = (bf16[1,180,256]{2,1,0:T(8,128)(2,1)S(1)}, bf16[1,180,256]{2,1,0:T(8,128)(2,1)S(1)}, u32[]{:S(2)}, u32[]{:S(2)}) collective-permute-start(bf16[1,180,256]{2,1,0:T(8,128)(2,1)S(1)} %copy.64), channel_id=1, source_target_pairs={{8,0},{16,8},{24,16},{32,24},{40,32},{48,40},{56,48},{64,56},{72,6... | collective-permute-start | bytes 276488 | tf_op jit(solution)/shard_map/ppermute | solution.py:17
  14.6 8.6 %collective-permute-start = (bf16[1,180,256]{2,1,0:T(8,128)(2,1)S(1)}, bf16[1,180,256]{2,1,0:T(8,128)(2,1)S(1)}, u32[]{:S(2)}, u32[]{:S(2)}) collective-permute-start(bf16[1,180,256]{2,1,0:T(8,128)(2,1)S(1)} %copy.63), channel_id=1, source_target_pairs={{0,8},{8,16},{16,24},{24,32},{32,40},{40,48},{48,56},{56,64},{64,7... | collective-permute-start | bytes 276488 | tf_op jit(solution)/shard_map/ppermute | solution.py:16
  24.1 4.5 %collective-permute-start.2 = (bf16[42,1,256]{2,0,1:T(8,128)(2,1)S(1)}, bf16[42,1,256]{2,0,1:T(8,128)(2,1)S(1)}, u32[]{:S(2)}, u32[]{:S(2)}) collective-permute-start(bf16[42,1,256]{2,0,1:T(8,128)(2,1)S(1)} %get-tuple-element.7), channel_id=1, source_target_pairs={{0,1},{1,2},{2,3},{3,4},{4,5},{5,6},{6,7},{7,0},{8,9},{9,10},{10,1... | collective-permute-start | bytes 64520 | tf_op jit(solution)/shard_map/ppermute | solution.py:16
  24.2 4.5 %collective-permute-start.3 = (bf16[42,1,256]{2,0,1:T(8,128)(2,1)S(1)}, bf16[42,1,256]{2,0,1:T(8,128)(2,1)S(1)}, u32[]{:S(2)}, u32[]{:S(2)}) collective-permute-start(bf16[42,1,256]{2,0,1:T(8,128)(2,1)S(1)} %get-tuple-element.8), channel_id=1, source_target_pairs={{1,0},{2,1},{3,2},{4,3},{5,4},{6,5},{7,6},{0,7},{9,8},{10,9},{11,1... | collective-permute-start | bytes 64520 | tf_op jit(solution)/shard_map/ppermute | solution.py:17
  31.8 2.0 copy-start.9
  50.1 9.1 %copy-start.4 = (bf16[256,128]{1,0:T(8,128)(2,1)S(1)}, bf16[256,128]{1,0:T(8,128)(2,1)}, u32[]{:S(2)}) copy-start(bf16[256,128]{1,0:T(8,128)(2,1)} %param.10) | copy-start | bytes 196612
  50.1 10.7 %copy-start.7 = (s32[16]{0:T(128)S(1)}, s32[16]{0:T(128)}, u32[]{:S(2)}) copy-start(s32[16]{0:T(128)} %param.13) | copy-start | bytes 196
  58.7 3.4 %copy-start.3 = (f32[720,128]{1,0:T(8,128)S(1)}, f32[720,128]{1,0:T(8,128)}, u32[]{:S(2)}) copy-start(f32[720,128]{1,0:T(8,128)} %param.12) | copy-start | bytes 1105924
  107.0 14.7 %collective-permute-start.4 = (bf16[2,1,720,128]{3,2,1,0:T(8,128)(2,1)S(1)}, bf16[2,1,720,128]{3,2,1,0:T(8,128)(2,1)S(1)}, u32[]{:S(2)}, u32[]{:S(2)}) collective-permute-start(bf16[2,1,720,128]{3,2,1,0:T(8,128)(2,1)S(1)} %get-tuple-element.5), channel_id=1, source_target_pairs={{0,8},{8,16},{16,24},{24,32},{32,40},{40,48},{48,56},{56,64},{64,7... | collective-permute-start | bytes 1105928 | tf_op jit(solution)/shard_map/ppermute | solution.py:16
  110.4 12.5 %collective-permute-start.5 = (bf16[2,1,720,128]{3,2,1,0:T(8,128)(2,1)S(1)}, bf16[2,1,720,128]{3,2,1,0:T(8,128)(2,1)S(1)}, u32[]{:S(2)}, u32[]{:S(2)}) collective-permute-start(bf16[2,1,720,128]{3,2,1,0:T(8,128)(2,1)S(1)} %get-tuple-element.6), channel_id=1, source_target_pairs={{8,0},{16,8},{24,16},{32,24},{40,32},{48,40},{56,48},{64,56},{72,6... | collective-permute-start | bytes 1105928 | tf_op jit(solution)/shard_map/ppermute | solution.py:17
  156.8 4.6 %copy-start.6 = (bf16[3,3,128,128]{3,2,1,0:T(8,128)(2,1)S(1)}, bf16[3,3,128,128]{3,2,1,0:T(8,128)(2,1)}, u32[]{:S(2)}) copy-start(bf16[3,3,128,128]{3,2,1,0:T(8,128)(2,1)} %param.14) | copy-start | bytes 884740
  156.8 4.6 %copy-start.8 = (pred[16,91]{0,1:T(8,128)(4,1)S(1)}, pred[16,91]{0,1:T(8,128)(4,1)}, u32[]{:S(2)}) copy-start(pred[16,91]{0,1:T(8,128)(4,1)} %constant.37) | copy-start | bytes 4372
  187.9 11.6 %copy-start.5 = (bf16[720,720]{1,0:T(8,128)(2,1)S(1)}, bf16[720,720]{1,0:T(8,128)(2,1)}, u32[]{:S(2)}) copy-start(bf16[720,720]{1,0:T(8,128)(2,1)} %param.15) | copy-start | bytes 3110404
  199.4 12.3 %copy-start.1 = (bf16[3,3,256,256]{3,2,1,0:T(8,128)(2,1)S(1)}, bf16[3,3,256,256]{3,2,1,0:T(8,128)(2,1)}, u32[]{:S(2)}) copy-start(bf16[3,3,256,256]{3,2,1,0:T(8,128)(2,1)} %param.9) | copy-start | bytes 3538948
Sparse Core Ops, SparseCore 0:
  60.9 31.4 all-gather.1
where the time goes:
time: 223 us; the launch traced here: 219 us
  other arithmetic  47.8 us (21%)
  local copies, waits for them, and re-layouts  47 us (21%)
  waiting for transfers between devices  46 us (21%)
  matrix products  45 us (20%)
  starting transfers between devices  19.1 us (9%)
  between operations  13.9 us (6%)
    conv_general_dilated x2, matrix products, conv_three(): lax.conv_general_dilated(batched, weight, (1, 1), 'VALID', dimension_numb...  30.8 us
    all_gather x1, waiting for transfers between devices, shards(): lax.all_gather(flat.astype(jnp.bfloat16).reshape(pooled.shape[0], pooled....  30 us
    conv_general_dilated x5, local copies, waits for them, and re-layouts, conv_three(): lax.conv_general_dilated(batched, weight, (1, 1), 'VALID', dimension_numb...  17.9 us
    convert_element_type x2, local copies, waits for them, and re-layouts, shards(): hidden = jax.nn.gelu(conv_three(padded_head, w_head)).astype(jnp.bfloat16)  16.7 us
    ppermute x3, waiting for transfers between devices, extended(): before = lax.ppermute(last, axis, up)  14.6 us
    ppermute x3, starting transfers between devices, extended(): after = lax.ppermute(initial, axis, down)  13.7 us
    concatenate x1, other arithmetic, wrap_columns(): jnp.concatenate([field[..., -1:, :], field, field[..., :1, :]], axis=-2)  13 us
    dot_general x1, matrix products, shards(): jnp.einsum('ij,bajc->baic', zonal_mix, hidden, preferred_element_type=jnp...  12.3 us
  transfers between devices with their start and end apart: 7, of which 6 were waited for; matrix products, arithmetic and copies ran while one was open for 1% of the time, Pallas kernels for 0%

commit v1 on v0

--- a/solution.py
+++ b/solution.py
@@ -1,9 +1,14 @@
+import functools
+
 import jax
 import jax.numpy as jnp
 from jax import lax
+from jax.experimental import pallas as pl
+from jax.experimental.pallas import tpu as pltpu
 from jax.sharding import PartitionSpec as P
 
 LEAD_DEV = 2
+HEAD_ROWS = 4
 
 
 def extended(x, sides, width, wrap):
@@ -39,15 +44,54 @@
     return summed * 0.25
 
 
-def wrap_columns(field):
-    return jnp.concatenate([field[..., -1:, :], field, field[..., :1, :]], axis=-2)
+def head_kernel(valid_ref, band_ref, scale_ref, shift_ref, w_ref, mix_ref, out_ref):
+    block = pl.program_id(1)
+    cols = band_ref.shape[1]
+    width = band_ref.shape[2]
+    gain = 1.0 + scale_ref[0]
+    shift = shift_ref[0]
+
+    def modulated(row):
+        value = (band_ref[row].astype(jnp.float32) * gain + shift).astype(jnp.bfloat16)
+        return jnp.where(valid_ref[row] > 0, value, jnp.zeros_like(value))
+
+    def one_row(j, carry):
+        row = block * HEAD_ROWS + j
+        rows = [modulated(row + k) for k in range(3)]
+        stacked = jnp.concatenate(rows, axis=-1)
+        taps = jnp.dot(stacked, w_ref[...], preferred_element_type=jnp.float32)
+        conv = (
+            pltpu.roll(taps[:, :width], 1, 0)
+            + taps[:, width : 2 * width]
+            + pltpu.roll(taps[:, 2 * width :], cols - 1, 0)
+        )
+        hidden = jax.nn.gelu(conv).astype(jnp.bfloat16)
+        mixed = jnp.dot(mix_ref[...], hidden, preferred_element_type=jnp.float32)
+        out_ref[0, j] = (rows[1].astype(jnp.float32) + mixed).astype(out_ref.dtype)
+        return carry
+
+    lax.fori_loop(0, HEAD_ROWS, one_row, 0)
 
 
-def modulate(projected, scales, shifts):
-    widened = projected.astype(jnp.float32)[None]
-    return (widened * (1.0 + scales[:, None, None, :]) + shifts[:, None, None, :]).astype(
-        jnp.bfloat16
-    )
+def head(valid, band, scales, shifts, w_all, zonal_mix):
+    halo_rows, cols, width = band.shape
+    rows = halo_rows - 2
+    leads = scales.shape[0]
+    return pl.pallas_call(
+        head_kernel,
+        out_shape=jax.ShapeDtypeStruct((leads, rows, cols, width), jnp.bfloat16),
+        grid=(leads, rows // HEAD_ROWS),
+        in_specs=[
+            pl.BlockSpec(memory_space=pltpu.SMEM),
+            pl.BlockSpec((halo_rows, cols, width), lambda l, b: (0, 0, 0)),
+            pl.BlockSpec((1, 1, width), lambda l, b: (l, 0, 0)),
+            pl.BlockSpec((1, 1, width), lambda l, b: (l, 0, 0)),
+            pl.BlockSpec((3 * width, 3 * width), lambda l, b: (0, 0)),
+            pl.BlockSpec((cols, cols), lambda l, b: (0, 0)),
+        ],
+        out_specs=pl.BlockSpec((1, HEAD_ROWS, cols, width), lambda l, b: (l, b, 0, 0)),
+        compiler_params=pltpu.CompilerParams(vmem_limit_bytes=48 * 1024 * 1024),
+    )(valid, band, scales[:, None, :], shifts[:, None, :], w_all, zonal_mix)
 
 
 def shards(inputs, w_enc, w_proj, film_scale, film_shift, lead_ids, w_head, zonal_mix):
@@ -60,25 +104,17 @@
     lon_group = lax.axis_index("lon")
     my_rows = lax.dynamic_slice_in_dim(lead_ids, lon_group * LEAD_DEV, LEAD_DEV)
     flat = jnp.dot(pooled.reshape(-1, channels), w_proj, preferred_element_type=jnp.float32)
-    band_proj = lax.all_gather(
-        flat.astype(jnp.bfloat16).reshape(pooled.shape[0], pooled.shape[1], head_width),
-        "lon",
-        axis=1,
-        tiled=True,
-    )
-    onehot = (my_rows[:, None] == jnp.arange(film_scale.shape[0], dtype=jnp.int32)[None, :]).astype(
-        jnp.float32
-    )
-    scales = jnp.dot(onehot, film_scale, precision=lax.Precision.HIGHEST)
-    shifts = jnp.dot(onehot, film_shift, precision=lax.Precision.HIGHEST)
-    scales, shifts = (scales, shifts)
-    with_band = None
-    modulated = modulate(band_proj, scales, shifts)
-    with_band = extended(modulated, (("lat", 1),), 1, False)
-    padded_head = wrap_columns(with_band)
-    hidden = jax.nn.gelu(conv_three(padded_head, w_head)).astype(jnp.bfloat16)
-    mixed = jnp.einsum("ij,bajc->baic", zonal_mix, hidden, preferred_element_type=jnp.float32)
-    return (modulated.astype(jnp.float32) + mixed).astype(jnp.bfloat16)
+    tile = flat.astype(jnp.bfloat16).reshape(pooled.shape[0], pooled.shape[1], head_width)
+    tile = extended(tile, (("lat", 0),), 1, False)
+    band = lax.all_gather(tile, "lon", axis=1, tiled=True)
+    scales = jnp.take(film_scale, my_rows, axis=0)
+    shifts = jnp.take(film_shift, my_rows, axis=0)
+    lat = lax.axis_index("lat")
+    halo_rows = band.shape[0]
+    index = jnp.arange(halo_rows, dtype=jnp.int32)
+    valid = ((index > 0) | (lat > 0)) & ((index < halo_rows - 1) | (lat < lax.axis_size("lat") - 1))
+    w_all = jnp.transpose(w_head, (0, 2, 1, 3)).reshape(3 * head_width, 3 * head_width)
+    return head(valid.astype(jnp.int32), band, scales, shifts, w_all, zonal_mix)
 
 
 def solution(mesh):

time: 223 us -> 189 us (0.85)
  Pallas kernels: 0 us -> 43.4 us
  local copies, waits for them, and re-layouts: 47 us -> 11.8 us
  other arithmetic: 47.8 us -> 16.7 us
  waiting for transfers between devices: 46 us -> 34.4 us
  matrix products: 45 us -> 48.1 us
    pallas_call x0 -> x1, Pallas kernels: none -> 43.4 us  [head(): pl.pallas_call(head_kernel, out_shape=jax.ShapeDtypeStruct((leads, rows,...]
    conv_general_dilated x5 -> x0, local copies, waits for them, and re-layouts: 17.9 us -> none  [conv_three(): lax.conv_general_dilated(batched, weight, (1, 1), 'VALID', dimension_numb...]
    conv_general_dilated x2 -> x1, matrix products: 30.8 us -> 47.7 us  [conv_three(): lax.conv_general_dilated(batched, weight, (1, 1), 'VALID', dimension_numb...]
    convert_element_type x2 -> x0, local copies, waits for them, and re-layouts: 16.7 us -> none  [shards(): hidden = jax.nn.gelu(conv_three(padded_head, w_head)).astype(jnp.bfloat16)]
    dot_general x3 -> x0, matrix products: 13.8 us -> none  [the longest x1 12.3 us: shards(): jnp.einsum('ij,bajc->baic', zonal_mix, hidden, preferred_element_type=jnp...]
    convert_element_type x2 -> x1, other arithmetic: 13.4 us -> 0.01 us  [shards(): return head(valid.astype(jnp.int32), band, scales, shifts, w_all, zonal_mix)]
    ppermute x3, waiting for transfers between devices: 14.6 us -> 2.45 us  [extended(): before = lax.ppermute(last, axis, up)]
    concatenate x1, other arithmetic: 13 us -> 1.15 us  [extended(): x = jnp.concatenate([before, x, after], axis=dim)]
  transfers between devices with their start and end apart: 7 -> 7, of which waited for: 6 -> 4; matrix products, arithmetic and copies ran while one was open for 1% -> 4% of each run, Pallas kernels for 0% -> 0%
where the time goes in v1:
time: 189 us; the launch traced here: 187 us
  matrix products  48.1 us (25%)
  Pallas kernels  43.4 us (23%)
  waiting for transfers between devices  34.4 us (18%)
  starting transfers between devices  19 us (10%)
  other arithmetic  16.7 us (9%)
  between operations  13.7 us (7%)
  local copies, waits for them, and re-layouts  11.8 us (6%)
    conv_general_dilated x1, matrix products, conv_three(): lax.conv_general_dilated(batched, weight, (1, 1), 'VALID', dimension_numb...  47.7 us
    pallas_call x1, Pallas kernels, head(): pl.pallas_call(head_kernel, out_shape=jax.ShapeDtypeStruct((leads, rows,...  43.4 us
    all_gather x1, waiting for transfers between devices, shards(): band = lax.all_gather(tile, 'lon', axis=1, tiled=True)  30.8 us
    ppermute x3, starting transfers between devices, extended(): after = lax.ppermute(initial, axis, down)  12.6 us
    another operation x1, other arithmetic, pool_pairs(): lax.reduce_window(field, jnp.array(0, field.dtype), lax.add, (2, 2, 1), (...  8.37 us
    ppermute x3, starting transfers between devices, extended(): before = lax.ppermute(last, axis, up)  6.37 us
    mul x1, other arithmetic, shards(): encoded = jax.nn.gelu(conv_three(padded, w_enc))  4.63 us
  transfers between devices with their start and end apart: 7, of which 4 were waited for; matrix products, arithmetic and copies ran while one was open for 4% of the time, Pallas kernels for 0%

profile of v1, /device:TPU:24, one launch (start us, length us, event | category | flops | bytes accessed | tf_op | source)
XLA Modules:
  0.0 187.0 jit_solution(4670732836102742919)
XLA Ops:
  6.5 0.0 copy-start
  6.5 0.0 all-gather.2.cloned.1.call-start
  6.5 1.7 fusion.10
  8.3 3.8 %collective-permute-start = (bf16[1,180,256]{2,1,0:T(8,128)(2,1)S(1)}, bf16[1,180,256]{2,1,0:T(8,128)(2,1)S(1)}, u32[]{:S(2)}, u32[]{:S(2)}) collective-permute-start(bf16[1,180,256]{2,1,0:T(8,128)(2,1)S(1)} %copy.43), channel_id=1, source_target_pairs={{0,8},{8,16},{16,24},{24,32},{32,40},{40,48},{48,56},{56,64},{64,7... | collective-permute-start | bytes 276488 | tf_op jit(solution)/shard_map/ppermute | solution.py:21
  12.2 4.2 %collective-permute-start.1 = (bf16[1,180,256]{2,1,0:T(8,128)(2,1)S(1)}, bf16[1,180,256]{2,1,0:T(8,128)(2,1)S(1)}, u32[]{:S(2)}, u32[]{:S(2)}) collective-permute-start(bf16[1,180,256]{2,1,0:T(8,128)(2,1)S(1)} %copy.44), channel_id=1, source_target_pairs={{8,0},{16,8},{24,16},{32,24},{40,32},{48,40},{56,48},{64,56},{72,6... | collective-permute-start | bytes 276488 | tf_op jit(solution)/shard_map/ppermute | solution.py:22
  16.4 0.7 collective-permute-done
  17.1 2.8 %constant_dynamic-update-slice_fusion.1 = bf16[42,180,256]{2,1,0:T(8,128)(2,1)S(1)} fusion(bf16[42,180,256]{2,1,0:T(8,128)(2,1)S(1)} %constant_dynamic-update-slice_fusion.2, bf16[40,180,256]{2,0,1:T(8,128)(2,1)} %param.10), kind=kLoop, calls=%fused_computation.20 | loop fusion | bytes 7454720
  19.9 0.0 collective-permute-done.1
  20.0 0.1 fusion.9
  20.0 0.0 collective-permute-start.2
  20.1 2.9 %collective-permute-start.3 = (bf16[42,1,256]{2,1,0:T(2,128)(2,1)S(1)}, bf16[42,1,256]{2,1,0:T(2,128)(2,1)S(1)}, u32[]{:S(2)}, u32[]{:S(2)}) collective-permute-start(bf16[42,1,256]{2,1,0:T(2,128)(2,1)S(1)} %get-tuple-element.9), channel_id=1, source_target_pairs={{1,0},{2,1},{3,2},{4,3},{5,4},{6,5},{7,6},{0,7},{9,8},{10,9},{11,1... | collective-permute-start | bytes 64520 | tf_op jit(solution)/shard_map/ppermute | solution.py:22
  23.0 1.7 collective-permute-done.2
  24.7 0.0 collective-permute-done.3
  24.7 2.2 %maximum_bitcast_fusion = bf16[1,42,182,256]{3,2,1,0:T(8,128)(2,1)S(1)} fusion(bf16[42,1,256]{2,1,0:T(2,128)(2,1)S(1)} %collective-permute-done.3, bf16[42,180,256]{2,1,0:T(8,128)(2,1)S(1)} %constant_dynamic-update-slice_fusion, bf16[42,1,256]{2,1,0:T(2,128)(2,1)S(1)} %collective-permute-done.2), kind=kLoop, calls=%fused_computation.12 | loop fusion | flops 11741184 | bytes 7827456 | tf_op jit(solution)/shard_map/broadcast_in_dim | solution.py:28
  26.9 0.0 copy-done
  26.9 47.7 %fusion = f32[1,40,180,256]{3,0,2,1:T(1,128)S(1)} fusion(bf16[3,3,256,256]{3,2,1,0:T(8,128)(2,1)S(1)} %copy-done, bf16[1,42,182,256]{3,2,1,0:T(8,128)(2,1)S(1)} %maximum_bitcast_fusion), kind=kOutput, calls=%fused_computation.3 | convolution fusion | flops 8493465600 | bytes 12466176 | tf_op jit(solution)/shard_map/conv_general_dilated | solution.py:29
  74.6 4.6 %fusion.8 = f32[40,180,256]{2,0,1:T(8,128)} fusion(f32[1,40,180,256]{3,0,2,1:T(1,128)S(1)} %fusion), kind=kLoop, calls=%fused_computation.11 | loop fusion | flops 14745600 | bytes 14745600 | tf_op jit(solution)/shard_map/mul | solution.py:101
  79.2 8.4 %reduce_window.7 = f32[20,90,256]{2,0,1:T(8,128)S(1)} reduce-window(f32[40,180,256]{2,0,1:T(8,128)} %fusion.8, f32[]{:T(128)} %constant.13.clone.1), window={size=2x2x1 stride=2x2x1}, to_apply=%region_0.0 | reduce-window | flops 1382400 | bytes 9216004 | tf_op jit(solution)/shard_map/reduce_window | solution.py:41
  87.6 0.0 copy-start.3
  87.6 0.2 multiply_convert_fusion
  87.8 0.2 copy.31
  88.0 0.0 copy-start.4
  88.0 0.0 copy-start.2
  88.0 0.2 convert_element_type.15
  88.3 0.1 copy-done.3
  88.4 0.4 convolution_convert_fusion
  88.8 2.5 %collective-permute-start.4 = (bf16[1,90,128]{2,1,0:T(8,128)(2,1)S(1)}, bf16[1,90,128]{2,1,0:T(8,128)(2,1)S(1)}, u32[]{:S(2)}, u32[]{:S(2)}) collective-permute-start(bf16[1,90,128]{2,1,0:T(8,128)(2,1)S(1)} %get-tuple-element.12), channel_id=1, source_target_pairs={{0,8},{8,16},{16,24},{24,32},{32,40},{40,48},{48,56},{56,64},{64,7... | collective-permute-start | bytes 69128 | tf_op jit(solution)/shard_map/ppermute | solution.py:21
  91.4 5.5 %collective-permute-start.5 = (bf16[1,90,128]{2,1,0:T(8,128)(2,1)S(1)}, bf16[1,90,128]{2,1,0:T(8,128)(2,1)S(1)}, u32[]{:S(2)}, u32[]{:S(2)}) collective-permute-start(bf16[1,90,128]{2,1,0:T(8,128)(2,1)S(1)} %get-tuple-element.13), channel_id=1, source_target_pairs={{8,0},{16,8},{24,16},{32,24},{40,32},{48,40},{56,48},{64,56},{72,6... | collective-permute-start | bytes 69128 | tf_op jit(solution)/shard_map/ppermute | solution.py:22
  96.8 0.1 reshape.18
  97.0 0.2 copy.33
  97.2 0.0 collective-permute-done.4
  97.2 1.1 collective-permute-done.5
  98.4 1.1 pad_maximum_fusion
  99.5 0.0 all-gather.2.cloned.1.call-update
  99.5 0.0 copy-done.4
  99.6 0.1 compare_and_fusion
  99.6 1.5 gather_fusion
  101.2 1.5 gather_fusion.1
  102.7 0.0 copy-done.2
  102.8 0.3 copy.35
  103.1 0.1 broadcast_select_fusion
  103.2 0.0 copy-start.1
  103.2 30.8 %all-gather.2.cloned.1.call-done = bf16[22,720,128]{2,0,1:T(8,128)(2,1)} async-done(((bf16[22,90,128]{2,0,1:T(8,128)(2,1)}), bf16[22,720,128]{2,0,1:T(8,128)(2,1)}) %all-gather.2.cloned.1.call-update) | async-done | bytes 4055056 | tf_op jit(solution)/shard_map/all_gather | solution.py:109
  134.0 2.8 %copy.36.band_ref = bf16[22,720,128]{2,1,0:T(8,128)(2,1)S(1)} copy(bf16[22,720,128]{2,0,1:T(8,128)(2,1)} %all-gather.2.cloned.1.call-done) | data formatting | bytes 8110080 | tf_op jit(solution)/shard_map/all_gather | solution.py:109
  136.8 0.0 copy-done.1
  136.8 43.4 %shard_map.82 = bf16[2,20,720,128]{3,2,1,0:T(8,128)(2,1)} custom-call(s32[22]{0:T(128)S(1)} %and_convert_fusion.valid_ref, bf16[22,720,128]{2,1,0:T(8,128)(2,1)S(1)} %copy.36.band_ref, f32[2,1,128]{2,1,0:T(1,128)S(1)} %bitcast.21, f32[2,1,128]{2,1,0:T(1,128)S(1)} %bitcast.20, bf16[384,384]{1,0:T(8,128)(2,1)S(1)} %bitcast.19, bf16[720,720]{1,0:T(8,128)(2,1)S(1)} %copy-done.1), custom_call_target="tpu_custom_call" | custom-call | tf_op jit(solution)/shard_map/pallas_call | solution.py:80
  (10 shorter events, 0.2 us)
Async XLA Ops:
  6.5 20.3 %copy-start = (bf16[3,3,256,256]{3,2,1,0:T(8,128)(2,1)S(1)}, bf16[3,3,256,256]{3,2,1,0:T(8,128)(2,1)}, u32[]{:S(2)}) copy-start(bf16[3,3,256,256]{3,2,1,0:T(8,128)(2,1)} %param.11) | copy-start | bytes 3538948
  6.5 127.5 %all-gather.2.cloned.1.call-start = ((), (), s32[]{:S(2)}) async-start(), calls=%async_computation | async-start | bytes 4976640 | tf_op jit(solution)/shard_map/all_gather | solution.py:109
  8.3 8.8 %collective-permute-start = (bf16[1,180,256]{2,1,0:T(8,128)(2,1)S(1)}, bf16[1,180,256]{2,1,0:T(8,128)(2,1)S(1)}, u32[]{:S(2)}, u32[]{:S(2)}) collective-permute-start(bf16[1,180,256]{2,1,0:T(8,128)(2,1)S(1)} %copy.43), channel_id=1, source_target_pairs={{0,8},{8,16},{16,24},{24,32},{32,40},{40,48},{48,56},{56,64},{64,7... | collective-permute-start | bytes 276488 | tf_op jit(solution)/shard_map/ppermute | solution.py:21
  12.2 7.8 %collective-permute-start.1 = (bf16[1,180,256]{2,1,0:T(8,128)(2,1)S(1)}, bf16[1,180,256]{2,1,0:T(8,128)(2,1)S(1)}, u32[]{:S(2)}, u32[]{:S(2)}) collective-permute-start(bf16[1,180,256]{2,1,0:T(8,128)(2,1)S(1)} %copy.44), channel_id=1, source_target_pairs={{8,0},{16,8},{24,16},{32,24},{40,32},{48,40},{56,48},{64,56},{72,6... | collective-permute-start | bytes 276488 | tf_op jit(solution)/shard_map/ppermute | solution.py:22
  20.0 4.7 %collective-permute-start.2 = (bf16[42,1,256]{2,1,0:T(2,128)(2,1)S(1)}, bf16[42,1,256]{2,1,0:T(2,128)(2,1)S(1)}, u32[]{:S(2)}, u32[]{:S(2)}) collective-permute-start(bf16[42,1,256]{2,1,0:T(2,128)(2,1)S(1)} %get-tuple-element.8), channel_id=1, source_target_pairs={{0,1},{1,2},{2,3},{3,4},{4,5},{5,6},{6,7},{7,0},{8,9},{9,10},{10,1... | collective-permute-start | bytes 64520 | tf_op jit(solution)/shard_map/ppermute | solution.py:21
  20.1 4.6 %collective-permute-start.3 = (bf16[42,1,256]{2,1,0:T(2,128)(2,1)S(1)}, bf16[42,1,256]{2,1,0:T(2,128)(2,1)S(1)}, u32[]{:S(2)}, u32[]{:S(2)}) collective-permute-start(bf16[42,1,256]{2,1,0:T(2,128)(2,1)S(1)} %get-tuple-element.9), channel_id=1, source_target_pairs={{1,0},{2,1},{3,2},{4,3},{5,4},{6,5},{7,6},{0,7},{9,8},{10,9},{11,1... | collective-permute-start | bytes 64520 | tf_op jit(solution)/shard_map/ppermute | solution.py:22
  87.6 0.8 copy-start.3
  88.0 11.6 %copy-start.4 = (s32[16]{0:T(128)S(1)}, s32[16]{0:T(128)}, u32[]{:S(2)}) copy-start(s32[16]{0:T(128)} %param.15) | copy-start | bytes 196
  88.0 14.7 %copy-start.2 = (bf16[3,3,128,128]{3,2,1,0:T(8,128)(2,1)S(1)}, bf16[3,3,128,128]{3,2,1,0:T(8,128)(2,1)}, u32[]{:S(2)}) copy-start(bf16[3,3,128,128]{3,2,1,0:T(8,128)(2,1)} %param.16) | copy-start | bytes 884740
  88.8 8.3 %collective-permute-start.4 = (bf16[1,90,128]{2,1,0:T(8,128)(2,1)S(1)}, bf16[1,90,128]{2,1,0:T(8,128)(2,1)S(1)}, u32[]{:S(2)}, u32[]{:S(2)}) collective-permute-start(bf16[1,90,128]{2,1,0:T(8,128)(2,1)S(1)} %get-tuple-element.12), channel_id=1, source_target_pairs={{0,8},{8,16},{16,24},{24,32},{32,40},{40,48},{48,56},{56,64},{64,7... | collective-permute-start | bytes 69128 | tf_op jit(solution)/shard_map/ppermute | solution.py:21
  91.4 7.0 %collective-permute-start.5 = (bf16[1,90,128]{2,1,0:T(8,128)(2,1)S(1)}, bf16[1,90,128]{2,1,0:T(8,128)(2,1)S(1)}, u32[]{:S(2)}, u32[]{:S(2)}) collective-permute-start(bf16[1,90,128]{2,1,0:T(8,128)(2,1)S(1)} %get-tuple-element.13), channel_id=1, source_target_pairs={{8,0},{16,8},{24,16},{32,24},{40,32},{48,40},{56,48},{64,56},{72,6... | collective-permute-start | bytes 69128 | tf_op jit(solution)/shard_map/ppermute | solution.py:22
  103.2 33.6 %copy-start.1 = (bf16[720,720]{1,0:T(8,128)(2,1)S(1)}, bf16[720,720]{1,0:T(8,128)(2,1)}, u32[]{:S(2)}) copy-start(bf16[720,720]{1,0:T(8,128)(2,1)} %mix_ref.1) | copy-start | bytes 3110404
Sparse Core Ops, SparseCore 0:
  99.7 34.2 all-gather.1

commit v2 on v1

--- a/solution.py
+++ b/solution.py
@@ -42,6 +42,56 @@
         field, jnp.array(0, field.dtype), lax.add, (2, 2, 1), (2, 2, 1), "VALID"
     )
     return summed * 0.25
+
+
+def encoder_kernel(x_ref, w_ref, proj_ref, out_ref, pair_ref):
+    cols = x_ref.shape[1]
+    width = x_ref.shape[2]
+    pooled_cols = out_ref.shape[1]
+
+    def encoded(row):
+        stacked = jnp.concatenate([x_ref[row + k] for k in range(3)], axis=-1)
+        taps = jnp.dot(stacked, w_ref[...], preferred_element_type=jnp.float32)
+        conv = (
+            taps[:, :width]
+            + pltpu.roll(taps[:, width : 2 * width], cols - 1, 0)
+            + pltpu.roll(taps[:, 2 * width :], cols - 2, 0)
+        )
+        return jax.nn.gelu(conv)
+
+    def one_row(p, carry):
+        pair = encoded(2 * p) + encoded(2 * p + 1)
+        lanes = pair_ref.shape[2]
+        chunks = []
+        for c in range(width // lanes):
+            pair_ref[c, pl.ds(0, cols)] = pair[:, c * lanes : (c + 1) * lanes]
+            pair_ref[c, pl.ds(cols, 8)] = jnp.zeros((8, lanes), jnp.float32)
+            half = pair_ref.shape[1] // 2
+            chunks.append(
+                pair_ref[c, pl.ds(0, half, stride=2)] + pair_ref[c, pl.ds(1, half, stride=2)]
+            )
+        summed = jnp.concatenate(chunks, axis=-1)
+        pooled = (summed * 0.25).astype(jnp.bfloat16)
+        projected = jnp.dot(pooled, proj_ref[...], preferred_element_type=jnp.float32)
+        out_ref[p] = projected[:pooled_cols].astype(out_ref.dtype)
+        return carry
+
+    lax.fori_loop(0, out_ref.shape[0], one_row, 0)
+
+
+def encoder(padded, w_enc, w_proj):
+    rows, cols, width = padded.shape
+    pooled_rows, pooled_cols = (rows - 2) // 2, (cols - 4) // 2
+    w_all = jnp.transpose(w_enc, (0, 2, 1, 3)).reshape(3 * width, 3 * width)
+    vmem = pl.BlockSpec(memory_space=pltpu.VMEM)
+    return pl.pallas_call(
+        encoder_kernel,
+        out_shape=jax.ShapeDtypeStruct((pooled_rows, pooled_cols, w_proj.shape[1]), jnp.bfloat16),
+        in_specs=[vmem, vmem, vmem],
+        out_specs=vmem,
+        scratch_shapes=[pltpu.VMEM((width // 128, cols + 8, 128), jnp.float32)],
+        compiler_params=pltpu.CompilerParams(vmem_limit_bytes=48 * 1024 * 1024),
+    )(padded, w_all, w_proj)
 
 
 def head_kernel(valid_ref, band_ref, scale_ref, shift_ref, w_ref, mix_ref, out_ref):
@@ -98,13 +148,11 @@
     lat_rows, lon_cols, channels = inputs.shape
     with_rows = extended(inputs, (("lat", 0),), 1, False)
     padded = extended(with_rows, (("lon", 1),), 1, True)
-    encoded = jax.nn.gelu(conv_three(padded, w_enc))
-    pooled = pool_pairs(encoded).astype(jnp.bfloat16)
+    padded = jnp.pad(padded, ((0, 0), (0, 2), (0, 0)))
+    tile = encoder(padded, w_enc, w_proj)
     head_width = w_proj.shape[1]
     lon_group = lax.axis_index("lon")
     my_rows = lax.dynamic_slice_in_dim(lead_ids, lon_group * LEAD_DEV, LEAD_DEV)
-    flat = jnp.dot(pooled.reshape(-1, channels), w_proj, preferred_element_type=jnp.float32)
-    tile = flat.astype(jnp.bfloat16).reshape(pooled.shape[0], pooled.shape[1], head_width)
     tile = extended(tile, (("lat", 0),), 1, False)
     band = lax.all_gather(tile, "lon", axis=1, tiled=True)
     scales = jnp.take(film_scale, my_rows, axis=0)

time: 189 us -> 144 us (0.76)
  matrix products: 48.1 us -> 0 us
  Pallas kernels: 43.4 us -> 60.1 us
  other arithmetic: 16.7 us -> 2.48 us
    conv_general_dilated x1 -> x0, matrix products: 47.7 us -> none  [conv_three(): lax.conv_general_dilated(batched, weight, (1, 1), 'VALID', dimension_numb...]
    pallas_call x0 -> x1, Pallas kernels: none -> 16.6 us  [encoder(): pl.pallas_call(encoder_kernel, out_shape=jax.ShapeDtypeStruct((pooled_row...]
    another operation x1 -> x0, other arithmetic: 8.37 us -> none  [pool_pairs(): lax.reduce_window(field, jnp.array(0, field.dtype), lax.add, (2, 2, 1), (...]
    mul x1 -> x0, other arithmetic: 4.63 us -> none  [shards(): encoded = jax.nn.gelu(conv_three(padded, w_enc))]
    broadcast_in_dim x1 -> x0, other arithmetic: 2.15 us -> none  [conv_three(): batched = padded if padded.ndim == 4 else padded[None]]
  transfers between devices with their start and end apart: 7 -> 7, of which waited for: 4 -> 4; matrix products, arithmetic and copies ran while one was open for 4% -> 5% of each run, Pallas kernels for 0% -> 0%
where the time goes in v2:
time: 144 us; the launch traced here: 142 us
  Pallas kernels  60.1 us (42%)
  waiting for transfers between devices  34.5 us (24%)
  starting transfers between devices  19 us (13%)
  between operations  13.6 us (9%)
  local copies, waits for them, and re-layouts  12.2 us (8%)
  other arithmetic  2.48 us (2%)
    pallas_call x1, Pallas kernels, head(): pl.pallas_call(head_kernel, out_shape=jax.ShapeDtypeStruct((leads, rows,...  43.4 us
    all_gather x1, waiting for transfers between devices, shards(): band = lax.all_gather(tile, 'lon', axis=1, tiled=True)  31.8 us
    pallas_call x1, Pallas kernels, encoder(): pl.pallas_call(encoder_kernel, out_shape=jax.ShapeDtypeStruct((pooled_row...  16.6 us
    ppermute x3, starting transfers between devices, extended(): after = lax.ppermute(initial, axis, down)  12.7 us
    ppermute x3, starting transfers between devices, extended(): before = lax.ppermute(last, axis, up)  6.27 us
    unnamed x18, local copies, waits for them, and re-layouts  3.27 us
  transfers between devices with their start and end apart: 7, of which 4 were waited for; matrix products, arithmetic and copies ran while one was open for 5% of the time, Pallas kernels for 0%

profile of v2, /device:TPU:24, one launch (start us, length us, event | category | flops | bytes accessed | tf_op | source)
XLA Modules:
  0.0 141.8 jit_solution(5574925796314078036)
XLA Ops:
  6.5 0.0 copy-start
  6.5 0.0 all-gather.2.cloned.1.call-start
  6.5 1.7 %fusion.6 = (bf16[1,180,256]{2,0,1:T(2,128)(2,1)S(1)}, bf16[1,180,256]{2,0,1:T(2,128)(2,1)S(1)}) fusion(bf16[40,180,256]{2,0,1:T(8,128)(2,1)} %param.10), kind=kLoop, calls=%fused_computation.20 | loop fusion | bytes 368640 | tf_op jit(solution)/shard_map/slice | solution.py:20
  8.3 3.8 %collective-permute-start = (bf16[1,180,256]{2,1,0:T(8,128)(2,1)S(1)}, bf16[1,180,256]{2,1,0:T(8,128)(2,1)S(1)}, u32[]{:S(2)}, u32[]{:S(2)}) collective-permute-start(bf16[1,180,256]{2,1,0:T(8,128)(2,1)S(1)} %copy.30), channel_id=1, source_target_pairs={{0,8},{8,16},{16,24},{24,32},{32,40},{40,48},{48,56},{56,64},{64,7... | collective-permute-start | bytes 276488 | tf_op jit(solution)/shard_map/ppermute | solution.py:21
  12.1 4.2 %collective-permute-start.1 = (bf16[1,180,256]{2,1,0:T(8,128)(2,1)S(1)}, bf16[1,180,256]{2,1,0:T(8,128)(2,1)S(1)}, u32[]{:S(2)}, u32[]{:S(2)}) collective-permute-start(bf16[1,180,256]{2,1,0:T(8,128)(2,1)S(1)} %copy.31), channel_id=1, source_target_pairs={{8,0},{16,8},{24,16},{32,24},{40,32},{48,40},{56,48},{64,56},{72,6... | collective-permute-start | bytes 276488 | tf_op jit(solution)/shard_map/ppermute | solution.py:22
  16.3 0.7 collective-permute-done
  17.1 0.0 copy-start.3
  17.1 2.9 %constant_dynamic-update-slice_fusion.1 = bf16[42,180,256]{2,1,0:T(8,128)(2,1)S(1)} fusion(bf16[42,180,256]{2,1,0:T(8,128)(2,1)S(1)} %constant_dynamic-update-slice_fusion.2, bf16[40,180,256]{2,0,1:T(8,128)(2,1)} %param.10), kind=kLoop, calls=%fused_computation.11 | loop fusion | bytes 7454720
  20.0 0.0 collective-permute-done.1
  20.0 0.1 fusion.5
  20.1 0.0 collective-permute-start.2
  20.1 2.9 %collective-permute-start.3 = (bf16[42,1,256]{2,1,0:T(2,128)(2,1)S(1)}, bf16[42,1,256]{2,1,0:T(2,128)(2,1)S(1)}, u32[]{:S(2)}, u32[]{:S(2)}) collective-permute-start(bf16[42,1,256]{2,1,0:T(2,128)(2,1)S(1)} %get-tuple-element.9), channel_id=1, source_target_pairs={{1,0},{2,1},{3,2},{4,3},{5,4},{6,5},{7,6},{0,7},{9,8},{10,9},{11,1... | collective-permute-start | bytes 64520 | tf_op jit(solution)/shard_map/ppermute | solution.py:22
  23.1 0.0 copy-done.3
  23.1 1.0 copy.22
  24.1 0.3 copy.26
  24.4 0.0 copy-start.2
  24.4 0.4 collective-permute-done.2
  24.8 0.0 collective-permute-done.3
  24.8 2.2 %fusion.4.x_ref = bf16[42,184,256]{2,1,0:T(8,128)(2,1)S(1)} fusion(bf16[42,1,256]{2,1,0:T(2,128)(2,1)S(1)} %collective-permute-done.3, bf16[42,180,256]{2,1,0:T(8,128)(2,1)S(1)} %constant_dynamic-update-slice_fusion, bf16[42,1,256]{2,1,0:T(2,128)(2,1)S(1)} %collective-permute-done.2), kind=kLoop, calls=%fused_computation.7 | loop fusion | flops 19783680 | bytes 7870464 | tf_op jit(solution)/shard_map/concatenate | solution.py:23
  27.0 0.0 copy-done.2
  27.0 0.0 copy-start.5
  27.0 0.0 copy-start.4
  27.0 16.6 %shard_map.82 = bf16[20,90,128]{2,1,0:T(8,128)(2,1)S(1)} custom-call(bf16[42,184,256]{2,1,0:T(8,128)(2,1)S(1)} %fusion.4.x_ref, bf16[768,768]{1,0:T(8,128)(2,1)S(1)} %bitcast.12, bf16[256,128]{1,0:T(8,128)(2,1)S(1)} %copy-done.2), custom_call_target="tpu_custom_call" | custom-call | tf_op jit(solution)/shard_map/pallas_call | solution.py:87
  43.7 2.4 %collective-permute-start.4 = (bf16[1,90,128]{2,1,0:T(8,128)(2,1)S(1)}, bf16[1,90,128]{2,1,0:T(8,128)(2,1)S(1)}, u32[]{:S(2)}, u32[]{:S(2)}) collective-permute-start(bf16[1,90,128]{2,1,0:T(8,128)(2,1)S(1)} %get-tuple-element.12), channel_id=1, source_target_pairs={{0,8},{8,16},{16,24},{24,32},{32,40},{40,48},{48,56},{56,64},{64,7... | collective-permute-start | bytes 69128 | tf_op jit(solution)/shard_map/ppermute | solution.py:21
  46.1 5.6 %collective-permute-start.5 = (bf16[1,90,128]{2,1,0:T(8,128)(2,1)S(1)}, bf16[1,90,128]{2,1,0:T(8,128)(2,1)S(1)}, u32[]{:S(2)}, u32[]{:S(2)}) collective-permute-start(bf16[1,90,128]{2,1,0:T(8,128)(2,1)S(1)} %get-tuple-element.13), channel_id=1, source_target_pairs={{8,0},{16,8},{24,16},{32,24},{40,32},{48,40},{56,48},{64,56},{72,6... | collective-permute-start | bytes 69128 | tf_op jit(solution)/shard_map/ppermute | solution.py:22
  51.7 0.0 collective-permute-done.4
  51.7 1.5 %collective-permute-done.5 = bf16[1,90,128]{2,1,0:T(8,128)(2,1)S(1)} collective-permute-done((bf16[1,90,128]{2,1,0:T(8,128)(2,1)S(1)}, bf16[1,90,128]{2,1,0:T(8,128)(2,1)S(1)}, u32[]{:S(2)}, u32[]{:S(2)}) %collective-permute-start.5) | collective-permute-done | bytes 23072 | tf_op jit(solution)/shard_map/ppermute | solution.py:22
  53.2 0.1 pad_maximum_fusion
  53.3 1.0 copy.23
  54.3 0.0 all-gather.2.cloned.1.call-update
  54.3 0.0 copy-done.5
  54.3 0.1 compare_and_fusion
  54.4 0.0 copy-done
  54.4 0.6 gather_fusion.1
  55.0 1.5 %gather_fusion = f32[2,128]{1,0:T(2,128)S(1)} fusion(f32[720,128]{1,0:T(8,128)} %param.13, s32[1024]{0:T(1024)S(1)} %pad_clamp_fusion), kind=kCustom, calls=%fused_computation.clone | custom fusion | bytes 2056 | tf_op jit(solution)/shard_map/jit(_take)/gather | solution.py:158
  56.5 0.0 copy-done.4
  56.5 0.3 copy.24
  56.9 0.1 broadcast_select_fusion
  56.9 0.0 copy-start.1
  56.9 31.8 %all-gather.2.cloned.1.call-done = bf16[22,720,128]{2,0,1:T(8,128)(2,1)} async-done(((bf16[22,90,128]{2,0,1:T(8,128)(2,1)}), bf16[22,720,128]{2,0,1:T(8,128)(2,1)}) %all-gather.2.cloned.1.call-update) | async-done | bytes 4055056 | tf_op jit(solution)/shard_map/all_gather | solution.py:157
  88.8 2.8 %copy.25.band_ref = bf16[22,720,128]{2,1,0:T(8,128)(2,1)S(1)} copy(bf16[22,720,128]{2,0,1:T(8,128)(2,1)} %all-gather.2.cloned.1.call-done) | data formatting | bytes 8110080 | tf_op jit(solution)/shard_map/all_gather | solution.py:157
  91.5 0.0 copy-done.1
  91.5 43.4 %shard_map.83 = bf16[2,20,720,128]{3,2,1,0:T(8,128)(2,1)} custom-call(s32[22]{0:T(128)S(1)} %and_convert_fusion.valid_ref, bf16[22,720,128]{2,1,0:T(8,128)(2,1)S(1)} %copy.25.band_ref, f32[2,1,128]{2,1,0:T(1,128)S(1)} %bitcast.15, f32[2,1,128]{2,1,0:T(1,128)S(1)} %bitcast.14, bf16[384,384]{1,0:T(8,128)(2,1)S(1)} %bitcast.13, bf16[720,720]{1,0:T(8,128)(2,1)S(1)} %copy-done.1), custom_call_target="tpu_custom_call" | custom-call | tf_op jit(solution)/shard_map/pallas_call | solution.py:130
  (8 shorter events, 0.1 us)
Async XLA Ops:
  6.5 47.9 %copy-start = (f32[720,128]{1,0:T(8,128)S(1)}, f32[720,128]{1,0:T(8,128)}, u32[]{:S(2)}) copy-start(f32[720,128]{1,0:T(8,128)} %param.14) | copy-start | bytes 1105924
  6.5 82.2 %all-gather.2.cloned.1.call-start = ((), (), s32[]{:S(2)}) async-start(), calls=%async_computation | async-start | bytes 4976640 | tf_op jit(solution)/shard_map/all_gather | solution.py:157
  8.3 8.8 %collective-permute-start = (bf16[1,180,256]{2,1,0:T(8,128)(2,1)S(1)}, bf16[1,180,256]{2,1,0:T(8,128)(2,1)S(1)}, u32[]{:S(2)}, u32[]{:S(2)}) collective-permute-start(bf16[1,180,256]{2,1,0:T(8,128)(2,1)S(1)} %copy.30), channel_id=1, source_target_pairs={{0,8},{8,16},{16,24},{24,32},{32,40},{40,48},{48,56},{56,64},{64,7... | collective-permute-start | bytes 276488 | tf_op jit(solution)/shard_map/ppermute | solution.py:21
  12.1 7.9 %collective-permute-start.1 = (bf16[1,180,256]{2,1,0:T(8,128)(2,1)S(1)}, bf16[1,180,256]{2,1,0:T(8,128)(2,1)S(1)}, u32[]{:S(2)}, u32[]{:S(2)}) collective-permute-start(bf16[1,180,256]{2,1,0:T(8,128)(2,1)S(1)} %copy.31), channel_id=1, source_target_pairs={{8,0},{16,8},{24,16},{32,24},{40,32},{48,40},{56,48},{64,56},{72,6... | collective-permute-start | bytes 276488 | tf_op jit(solution)/shard_map/ppermute | solution.py:22
  17.1 6.0 %copy-start.3 = (bf16[3,3,256,256]{3,2,1,0:T(8,128)(2,1)S(1)}, bf16[3,3,256,256]{3,2,1,0:T(8,128)(2,1)}, u32[]{:S(2)}) copy-start(bf16[3,3,256,256]{3,2,1,0:T(8,128)(2,1)} %param.11) | copy-start | bytes 3538948
  20.1 4.7 %collective-permute-start.2 = (bf16[42,1,256]{2,1,0:T(2,128)(2,1)S(1)}, bf16[42,1,256]{2,1,0:T(2,128)(2,1)S(1)}, u32[]{:S(2)}, u32[]{:S(2)}) collective-permute-start(bf16[42,1,256]{2,1,0:T(2,128)(2,1)S(1)} %get-tuple-element.8), channel_id=1, source_target_pairs={{0,1},{1,2},{2,3},{3,4},{4,5},{5,6},{6,7},{7,0},{8,9},{9,10},{10,1... | collective-permute-start | bytes 64520 | tf_op jit(solution)/shard_map/ppermute | solution.py:21
  20.1 4.6 %collective-permute-start.3 = (bf16[42,1,256]{2,1,0:T(2,128)(2,1)S(1)}, bf16[42,1,256]{2,1,0:T(2,128)(2,1)S(1)}, u32[]{:S(2)}, u32[]{:S(2)}) collective-permute-start(bf16[42,1,256]{2,1,0:T(2,128)(2,1)S(1)} %get-tuple-element.9), channel_id=1, source_target_pairs={{1,0},{2,1},{3,2},{4,3},{5,4},{6,5},{7,6},{0,7},{9,8},{10,9},{11,1... | collective-permute-start | bytes 64520 | tf_op jit(solution)/shard_map/ppermute | solution.py:22
  24.4 2.6 %copy-start.2 = (bf16[256,128]{1,0:T(8,128)(2,1)S(1)}, bf16[256,128]{1,0:T(8,128)(2,1)}, u32[]{:S(2)}) copy-start(bf16[256,128]{1,0:T(8,128)(2,1)} %proj_ref.1) | copy-start | bytes 196612
  27.0 27.3 %copy-start.5 = (s32[16]{0:T(128)S(1)}, s32[16]{0:T(128)}, u32[]{:S(2)}) copy-start(s32[16]{0:T(128)} %param.15) | copy-start | bytes 196
  27.0 29.5 %copy-start.4 = (bf16[3,3,128,128]{3,2,1,0:T(8,128)(2,1)S(1)}, bf16[3,3,128,128]{3,2,1,0:T(8,128)(2,1)}, u32[]{:S(2)}) copy-start(bf16[3,3,128,128]{3,2,1,0:T(8,128)(2,1)} %param.16) | copy-start | bytes 884740
  43.7 8.0 %collective-permute-start.4 = (bf16[1,90,128]{2,1,0:T(8,128)(2,1)S(1)}, bf16[1,90,128]{2,1,0:T(8,128)(2,1)S(1)}, u32[]{:S(2)}, u32[]{:S(2)}) collective-permute-start(bf16[1,90,128]{2,1,0:T(8,128)(2,1)S(1)} %get-tuple-element.12), channel_id=1, source_target_pairs={{0,8},{8,16},{16,24},{24,32},{32,40},{40,48},{48,56},{56,64},{64,7... | collective-permute-start | bytes 69128 | tf_op jit(solution)/shard_map/ppermute | solution.py:21
  46.1 7.1 %collective-permute-start.5 = (bf16[1,90,128]{2,1,0:T(8,128)(2,1)S(1)}, bf16[1,90,128]{2,1,0:T(8,128)(2,1)S(1)}, u32[]{:S(2)}, u32[]{:S(2)}) collective-permute-start(bf16[1,90,128]{2,1,0:T(8,128)(2,1)S(1)} %get-tuple-element.13), channel_id=1, source_target_pairs={{8,0},{16,8},{24,16},{32,24},{40,32},{48,40},{56,48},{64,56},{72,6... | collective-permute-start | bytes 69128 | tf_op jit(solution)/shard_map/ppermute | solution.py:22
  56.9 34.6 %copy-start.1 = (bf16[720,720]{1,0:T(8,128)(2,1)S(1)}, bf16[720,720]{1,0:T(8,128)(2,1)}, u32[]{:S(2)}) copy-start(bf16[720,720]{1,0:T(8,128)(2,1)} %mix_ref.1) | copy-start | bytes 3110404
Sparse Core Ops, SparseCore 0:
  54.4 34.2 all-gather.1

commit v3 on v2

--- a/solution.py
+++ b/solution.py
@@ -8,7 +8,7 @@
 from jax.sharding import PartitionSpec as P
 
 LEAD_DEV = 2
-HEAD_ROWS = 4
+HEAD_ROWS = 5
 
 
 def extended(x, sides, width, wrap):
@@ -94,54 +94,64 @@
     )(padded, w_all, w_proj)
 
 
-def head_kernel(valid_ref, band_ref, scale_ref, shift_ref, w_ref, mix_ref, out_ref):
-    block = pl.program_id(1)
-    cols = band_ref.shape[1]
-    width = band_ref.shape[2]
+def head_kernel(chunk, valid_ref, main_ref, next_ref, scale_ref, shift_ref, w_ref, mix_ref, *rest):
+    out_ref, mod_ref, hidden_ref = rest[-3:]
+    rows = main_ref.shape[0]
+    cols = main_ref.shape[1]
+    width = main_ref.shape[2]
     gain = 1.0 + scale_ref[0]
     shift = shift_ref[0]
-
-    def modulated(row):
-        value = (band_ref[row].astype(jnp.float32) * gain + shift).astype(jnp.bfloat16)
-        return jnp.where(valid_ref[row] > 0, value, jnp.zeros_like(value))
-
-    def one_row(j, carry):
-        row = block * HEAD_ROWS + j
-        rows = [modulated(row + k) for k in range(3)]
-        stacked = jnp.concatenate(rows, axis=-1)
+    for j in range(rows + 2):
+        source = main_ref[j] if j < rows else next_ref[j - rows]
+        value = (source.astype(jnp.float32) * gain + shift).astype(jnp.bfloat16)
+        keep = valid_ref[chunk * rows + j] > 0
+        mod_ref[j] = jnp.where(keep, value, jnp.zeros_like(value))
+    for j in range(rows):
+        stacked = jnp.concatenate([mod_ref[j + k] for k in range(3)], axis=-1)
         taps = jnp.dot(stacked, w_ref[...], preferred_element_type=jnp.float32)
         conv = (
             pltpu.roll(taps[:, :width], 1, 0)
             + taps[:, width : 2 * width]
             + pltpu.roll(taps[:, 2 * width :], cols - 1, 0)
         )
-        hidden = jax.nn.gelu(conv).astype(jnp.bfloat16)
-        mixed = jnp.dot(mix_ref[...], hidden, preferred_element_type=jnp.float32)
-        out_ref[0, j] = (rows[1].astype(jnp.float32) + mixed).astype(out_ref.dtype)
-        return carry
-
-    lax.fori_loop(0, HEAD_ROWS, one_row, 0)
+        hidden_ref[:, j * width : (j + 1) * width] = jax.nn.gelu(conv).astype(jnp.bfloat16)
+    mixed = jnp.dot(mix_ref[...], hidden_ref[...], preferred_element_type=jnp.float32)
+    for j in range(rows):
+        own = mod_ref[j + 1].astype(jnp.float32)
+        out_ref[0, j] = (own + mixed[:, j * width : (j + 1) * width]).astype(out_ref.dtype)
 
 
-def head(valid, band, scales, shifts, w_all, zonal_mix):
-    halo_rows, cols, width = band.shape
-    rows = halo_rows - 2
+def head(chunk, total_rows, previous, valid, main, following, scales, shifts, w_all, zonal_mix):
+    rows, cols, width = main.shape
     leads = scales.shape[0]
+    in_specs = [
+        pl.BlockSpec(memory_space=pltpu.SMEM),
+        pl.BlockSpec((rows, cols, width), lambda l: (0, 0, 0)),
+        pl.BlockSpec((2, cols, width), lambda l: (0, 0, 0)),
+        pl.BlockSpec((1, 1, width), lambda l: (l, 0, 0)),
+        pl.BlockSpec((1, 1, width), lambda l: (l, 0, 0)),
+        pl.BlockSpec((3 * width, 3 * width), lambda l: (0, 0)),
+        pl.BlockSpec((cols, cols), lambda l: (0, 0)),
+    ]
+    operands = [valid, main, following, scales[:, None, :], shifts[:, None, :], w_all, zonal_mix]
+    aliases = {}
+    if previous is not None:
+        in_specs.append(pl.BlockSpec(memory_space=pl.ANY))
+        operands.append(previous)
+        aliases = {len(operands) - 1: 0}
     return pl.pallas_call(
-        head_kernel,
-        out_shape=jax.ShapeDtypeStruct((leads, rows, cols, width), jnp.bfloat16),
-        grid=(leads, rows // HEAD_ROWS),
-        in_specs=[
-            pl.BlockSpec(memory_space=pltpu.SMEM),
-            pl.BlockSpec((halo_rows, cols, width), lambda l, b: (0, 0, 0)),
-            pl.BlockSpec((1, 1, width), lambda l, b: (l, 0, 0)),
-            pl.BlockSpec((1, 1, width), lambda l, b: (l, 0, 0)),
-            pl.BlockSpec((3 * width, 3 * width), lambda l, b: (0, 0)),
-            pl.BlockSpec((cols, cols), lambda l, b: (0, 0)),
+        functools.partial(head_kernel, chunk),
+        out_shape=jax.ShapeDtypeStruct((leads, total_rows, cols, width), jnp.bfloat16),
+        grid=(leads,),
+        in_specs=in_specs,
+        out_specs=pl.BlockSpec((1, rows, cols, width), lambda l: (l, chunk, 0, 0)),
+        scratch_shapes=[
+            pltpu.VMEM((rows + 2, cols, width), jnp.bfloat16),
+            pltpu.VMEM((cols, rows * width), jnp.bfloat16),
         ],
-        out_specs=pl.BlockSpec((1, HEAD_ROWS, cols, width), lambda l, b: (l, b, 0, 0)),
+        input_output_aliases=aliases,
         compiler_params=pltpu.CompilerParams(vmem_limit_bytes=48 * 1024 * 1024),
-    )(valid, band, scales[:, None, :], shifts[:, None, :], w_all, zonal_mix)
+    )(*operands)
 
 
 def shards(inputs, w_enc, w_proj, film_scale, film_shift, lead_ids, w_head, zonal_mix):
@@ -154,15 +164,25 @@
     lon_group = lax.axis_index("lon")
     my_rows = lax.dynamic_slice_in_dim(lead_ids, lon_group * LEAD_DEV, LEAD_DEV)
     tile = extended(tile, (("lat", 0),), 1, False)
-    band = lax.all_gather(tile, "lon", axis=1, tiled=True)
     scales = jnp.take(film_scale, my_rows, axis=0)
     shifts = jnp.take(film_shift, my_rows, axis=0)
     lat = lax.axis_index("lat")
-    halo_rows = band.shape[0]
+    halo_rows = tile.shape[0]
+    rows = halo_rows - 2
     index = jnp.arange(halo_rows, dtype=jnp.int32)
     valid = ((index > 0) | (lat > 0)) & ((index < halo_rows - 1) | (lat < lax.axis_size("lat") - 1))
+    valid = valid.astype(jnp.int32)
     w_all = jnp.transpose(w_head, (0, 2, 1, 3)).reshape(3 * head_width, 3 * head_width)
-    return head(valid.astype(jnp.int32), band, scales, shifts, w_all, zonal_mix)
+    chunks = rows // HEAD_ROWS
+    bands = [
+        lax.all_gather(tile[k * HEAD_ROWS : (k + 1) * HEAD_ROWS], "lon", axis=1, tiled=True)
+        for k in range(chunks)
+    ]
+    bands.append(lax.all_gather(tile[rows:], "lon", axis=1, tiled=True))
+    out = None
+    for k in range(chunks):
+        out = head(k, rows, out, valid, bands[k], bands[k + 1], scales, shifts, w_all, zonal_mix)
+    return out
 
 
 def solution(mesh):

time: 144 us -> 154 us (1.069)
  blocking collectives: 0 us -> 72.2 us
  waiting for transfers between devices: 34.5 us -> 0.31 us
  between operations: 13.6 us -> 0.34 us
  Pallas kernels: 60.1 us -> 47.3 us
  local copies, waits for them, and re-layouts: 12.2 us -> 9.28 us
  other arithmetic: 2.48 us -> 4.77 us
    all_gather x0 -> x5, blocking collectives: none -> 72.2 us  [the longest x4 58.6 us: shards(): lax.all_gather(tile[k * HEAD_ROWS:(k + 1) * HEAD_ROWS], 'lon', axis=1, ti...]
    all_gather x1 -> x0, waiting for transfers between devices: 31.8 us -> none  [shards(): band = lax.all_gather(tile, 'lon', axis=1, tiled=True)]
    pallas_call x1 -> x4, Pallas kernels: 43.4 us -> 30.6 us  [head(): pl.pallas_call(functools.partial(head_kernel, chunk), out_shape=jax.Shape...]
    all_gather x1 -> x5, local copies, waits for them, and re-layouts: 2.78 us -> 0.57 us  [the longest x4 0.52 us: shards(): lax.all_gather(tile[k * HEAD_ROWS:(k + 1) * HEAD_ROWS], 'lon', axis=1, ti...]
    concatenate x2 -> x3, other arithmetic: 2.31 us -> 3.95 us  [extended(): x = jnp.concatenate([before, x, after], axis=dim)]
  transfers between devices with their start and end apart: 7 -> 6, of which waited for: 4 -> 1; matrix products, arithmetic and copies ran while one was open for 5% -> 5% of each run, Pallas kernels for 0% -> 0%
where the time goes in v3:
time: 154 us; the launch traced here: 153 us
  blocking collectives  72.2 us (47%)
  Pallas kernels  47.3 us (31%)
  starting transfers between devices  19 us (12%)
  local copies, waits for them, and re-layouts  9.28 us (6%)
  other arithmetic  4.77 us (3%)
    all_gather x4, blocking collectives, shards(): lax.all_gather(tile[k * HEAD_ROWS:(k + 1) * HEAD_ROWS], 'lon', axis=1, ti...  58.6 us
    pallas_call x4, Pallas kernels, head(): pl.pallas_call(functools.partial(head_kernel, chunk), out_shape=jax.Shape...  30.6 us
    pallas_call x1, Pallas kernels, encoder(): pl.pallas_call(encoder_kernel, out_shape=jax.ShapeDtypeStruct((pooled_row...  16.7 us
    all_gather x1, blocking collectives, shards(): bands.append(lax.all_gather(tile[rows:], 'lon', axis=1, tiled=True))  13.6 us
    ppermute x3, starting transfers between devices, extended(): after = lax.ppermute(initial, axis, down)  13.2 us
    ppermute x3, starting transfers between devices, extended(): before = lax.ppermute(last, axis, up)  5.76 us
    concatenate x3, other arithmetic, extended(): x = jnp.concatenate([before, x, after], axis=dim)  3.95 us
    unnamed x18, local copies, waits for them, and re-layouts  3.28 us
  transfers between devices with their start and end apart: 6, of which 1 were waited for; matrix products, arithmetic and copies ran while one was open for 5% of the time, Pallas kernels for 0%

profile of v3, /device:TPU:24, one launch (start us, length us, event | category | flops | bytes accessed | tf_op | source)
XLA Modules:
  0.0 153.2 jit_solution(8631082082881781436)
XLA Ops:
  0.0 0.0 copy-start
  0.0 1.7 %fusion.6 = (bf16[1,180,256]{2,0,1:T(2,128)(2,1)S(1)}, bf16[1,180,256]{2,0,1:T(2,128)(2,1)S(1)}) fusion(bf16[40,180,256]{2,0,1:T(8,128)(2,1)} %param.10), kind=kLoop, calls=%fused_computation.21 | loop fusion | bytes 368640 | tf_op jit(solution)/shard_map/slice | solution.py:20
  1.7 3.8 %collective-permute-start = (bf16[1,180,256]{2,1,0:T(8,128)(2,1)S(1)}, bf16[1,180,256]{2,1,0:T(8,128)(2,1)S(1)}, u32[]{:S(2)}, u32[]{:S(2)}) collective-permute-start(bf16[1,180,256]{2,1,0:T(8,128)(2,1)S(1)} %copy.44), channel_id=1, source_target_pairs={{0,8},{8,16},{16,24},{24,32},{32,40},{40,48},{48,56},{56,64},{64,7... | collective-permute-start | bytes 276488 | tf_op jit(solution)/shard_map/ppermute | solution.py:21
  5.6 4.2 %collective-permute-start.1 = (bf16[1,180,256]{2,1,0:T(8,128)(2,1)S(1)}, bf16[1,180,256]{2,1,0:T(8,128)(2,1)S(1)}, u32[]{:S(2)}, u32[]{:S(2)}) collective-permute-start(bf16[1,180,256]{2,1,0:T(8,128)(2,1)S(1)} %copy.45), channel_id=1, source_target_pairs={{8,0},{16,8},{24,16},{32,24},{40,32},{48,40},{56,48},{64,56},{72,6... | collective-permute-start | bytes 276488 | tf_op jit(solution)/shard_map/ppermute | solution.py:22
  9.8 0.7 compare_and_fusion
  10.6 0.6 gather_fusion
  11.1 1.5 %gather_fusion.1 = f32[2,128]{1,0:T(2,128)S(1)} fusion(f32[720,128]{1,0:T(8,128)} %param.14, s32[1024]{0:T(1024)S(1)} %pad_clamp_fusion), kind=kCustom, calls=%fused_computation.1.clone | custom fusion | bytes 2056 | tf_op jit(solution)/shard_map/jit(_take)/gather | solution.py:168
  12.7 0.0 collective-permute-done
  12.7 0.0 copy-start.4
  12.7 2.9 %constant_dynamic-update-slice_fusion.1 = bf16[42,180,256]{2,1,0:T(8,128)(2,1)S(1)} fusion(bf16[42,180,256]{2,1,0:T(8,128)(2,1)S(1)} %constant_dynamic-update-slice_fusion.2, bf16[40,180,256]{2,0,1:T(8,128)(2,1)} %param.10), kind=kLoop, calls=%fused_computation.12 | loop fusion | bytes 7454720
  15.6 0.0 collective-permute-done.1
  15.6 0.0 copy-start.3
  15.6 0.1 fusion.5
  15.7 0.0 collective-permute-start.2
  15.7 2.9 %collective-permute-start.3 = (bf16[42,1,256]{2,1,0:T(2,128)(2,1)S(1)}, bf16[42,1,256]{2,1,0:T(2,128)(2,1)S(1)}, u32[]{:S(2)}, u32[]{:S(2)}) collective-permute-start(bf16[42,1,256]{2,1,0:T(2,128)(2,1)S(1)} %get-tuple-element.9), channel_id=1, source_target_pairs={{1,0},{2,1},{3,2},{4,3},{5,4},{6,5},{7,6},{0,7},{9,8},{10,9},{11,1... | collective-permute-start | bytes 64520 | tf_op jit(solution)/shard_map/ppermute | solution.py:22
  18.7 0.1 broadcast_select_fusion
  18.7 1.0 copy.25
  19.8 0.3 copy.40
  20.1 0.0 copy-start.2
  20.1 0.3 collective-permute-done.2
  20.4 0.0 collective-permute-done.3
  20.4 3.9 %fusion.4.x_ref = bf16[42,184,256]{2,1,0:T(8,128)(2,1)S(1)} fusion(bf16[42,1,256]{2,1,0:T(2,128)(2,1)S(1)} %collective-permute-done.3, bf16[42,180,256]{2,1,0:T(8,128)(2,1)} %copy-done.3, bf16[42,1,256]{2,1,0:T(2,128)(2,1)S(1)} %collective-permute-done.2), kind=kLoop, calls=%fused_computation.7 | loop fusion | flops 19783680 | bytes 7870464 | tf_op jit(solution)/shard_map/concatenate | solution.py:23
  24.3 0.0 copy-start.5
  24.3 16.7 %shard_map.82 = bf16[20,90,128]{2,1,0:T(8,128)(2,1)S(1)} custom-call(bf16[42,184,256]{2,1,0:T(8,128)(2,1)S(1)} %fusion.4.x_ref, bf16[768,768]{1,0:T(8,128)(2,1)S(1)} %bitcast.16, bf16[256,128]{1,0:T(8,128)(2,1)S(1)} %copy-done.2), custom_call_target="tpu_custom_call" | custom-call | tf_op jit(solution)/shard_map/pallas_call | solution.py:87
  41.0 1.9 %collective-permute-start.5 = (bf16[1,90,128]{2,1,0:T(8,128)(2,1)S(1)}, bf16[1,90,128]{2,1,0:T(8,128)(2,1)S(1)}, u32[]{:S(2)}, u32[]{:S(2)}) collective-permute-start(bf16[1,90,128]{2,1,0:T(8,128)(2,1)S(1)} %get-tuple-element.16), channel_id=1, source_target_pairs={{0,8},{8,16},{16,24},{24,32},{32,40},{40,48},{48,56},{56,64},{64,7... | collective-permute-start | bytes 69128 | tf_op jit(solution)/shard_map/ppermute | solution.py:21
  42.9 0.3 copy.28
  43.3 6.1 %collective-permute-start.4 = (bf16[1,90,128]{2,1,0:T(8,128)(2,1)S(1)}, bf16[1,90,128]{2,1,0:T(8,128)(2,1)S(1)}, u32[]{:S(2)}, u32[]{:S(2)}) collective-permute-start(bf16[1,90,128]{2,1,0:T(8,128)(2,1)S(1)} %get-tuple-element.17), channel_id=1, source_target_pairs={{8,0},{16,8},{24,16},{32,24},{40,32},{48,40},{56,48},{64,56},{72,6... | collective-permute-start | bytes 69128 | tf_op jit(solution)/shard_map/ppermute | solution.py:22
  49.3 0.0 collective-permute-done.5
  49.4 0.1 copy.30
  49.5 14.1 %all_gather.18 = bf16[5,720,128]{2,0,1:T(8,128)(2,1)S(1)} all-gather(bf16[5,90,128]{2,0,1:T(8,128)(2,1)S(1)} %copy.30), channel_id=1, replica_groups=mesh['lat'=16,'lon'=8] {'lon'}, dimensions={1}, use_global_device_ids=true | all-gather | bytes 1036800 | tf_op jit(solution)/shard_map/all_gather | solution.py:178
  63.6 0.1 copy.31
  63.6 14.5 %all_gather.19 = bf16[5,720,128]{2,0,1:T(8,128)(2,1)S(1)} all-gather(bf16[5,90,128]{2,0,1:T(8,128)(2,1)S(1)} %copy.31), channel_id=1, replica_groups=mesh['lat'=16,'lon'=8] {'lon'}, dimensions={1}, use_global_device_ids=true | all-gather | bytes 1036800 | tf_op jit(solution)/shard_map/all_gather | solution.py:178
  78.1 0.1 copy.29
  78.2 14.8 %all_gather.17 = bf16[5,720,128]{2,0,1:T(8,128)(2,1)S(1)} all-gather(bf16[5,90,128]{2,0,1:T(8,128)(2,1)S(1)} %copy.29), channel_id=1, replica_groups=mesh['lat'=16,'lon'=8] {'lon'}, dimensions={1}, use_global_device_ids=true | all-gather | bytes 1036800 | tf_op jit(solution)/shard_map/all_gather | solution.py:178
  92.9 0.1 copy.26
  93.0 15.2 %all_gather.15 = bf16[5,720,128]{2,0,1:T(8,128)(2,1)S(1)} all-gather(bf16[5,90,128]{2,0,1:T(8,128)(2,1)S(1)} %copy.26), channel_id=1, replica_groups=mesh['lat'=16,'lon'=8] {'lon'}, dimensions={1}, use_global_device_ids=true | all-gather | bytes 1036800 | tf_op jit(solution)/shard_map/all_gather | solution.py:178
  108.2 0.1 copy.34.next_ref.main_ref
  108.4 0.0 copy-start.1
  108.4 0.1 copy.32.main_ref
  108.5 0.1 copy.36.next_ref.main_ref
  108.6 0.1 copy.38.next_ref.main_ref
  108.8 0.0 collective-permute-done.4
  108.9 13.6 %all_gather.16 = bf16[2,720,128]{2,0,1:T(2,128)(2,1)S(1)} all-gather(bf16[2,90,128]{2,0,1:T(2,128)(2,1)S(1)} %copy.27), channel_id=1, replica_groups=mesh['lat'=16,'lon'=8] {'lon'}, dimensions={1}, use_global_device_ids=true | all-gather | bytes 414720 | tf_op jit(solution)/shard_map/all_gather | solution.py:181
  122.5 0.1 copy.39.next_ref
  122.5 7.8 %shard_map.83.rest_0_ = bf16[2,20,720,128]{3,2,1,0:T(8,128)(2,1)} custom-call(s32[22]{0:T(128)S(1)} %and_convert_fusion.valid_ref, bf16[5,720,128]{2,1,0:T(8,128)(2,1)S(1)} %copy.32.main_ref, bf16[5,720,128]{2,1,0:T(8,128)(2,1)S(1)} %copy.34.next_ref.main_ref, f32[2,1,128]{2,1,0:T(1,128)S(1)} %bitcast.21, f32[2,1,128]{2,1,0:T(1,128)S(1)} %bitcast.17, ...), custom_call_target="tpu_custom_call" | custom-call | tf_op jit(solution)/shard_map/pallas_call | solution.py:142
  130.4 7.6 %shard_map.84.rest_0_ = bf16[2,20,720,128]{3,2,1,0:T(8,128)(2,1)} custom-call(s32[22]{0:T(128)S(1)} %and_convert_fusion.valid_ref, bf16[5,720,128]{2,1,0:T(8,128)(2,1)S(1)} %copy.34.next_ref.main_ref, bf16[5,720,128]{2,1,0:T(8,128)(2,1)S(1)} %copy.36.next_ref.main_ref, f32[2,1,128]{2,1,0:T(1,128)S(1)} %bitcast.22, ...), custom_call_target="tpu_custom_call", output_to_operand_aliasing={{}: (7, {})} | custom-call | tf_op jit(solution)/shard_map/pallas_call | solution.py:142
  138.0 7.6 %shard_map.85.rest_0_ = bf16[2,20,720,128]{3,2,1,0:T(8,128)(2,1)} custom-call(s32[22]{0:T(128)S(1)} %and_convert_fusion.valid_ref, bf16[5,720,128]{2,1,0:T(8,128)(2,1)S(1)} %copy.36.next_ref.main_ref, bf16[5,720,128]{2,1,0:T(8,128)(2,1)S(1)} %copy.38.next_ref.main_ref, f32[2,1,128]{2,1,0:T(1,128)S(1)} %bitcast.23, ...), custom_call_target="tpu_custom_call", output_to_operand_aliasing={{}: (7, {})} | custom-call | tf_op jit(solution)/shard_map/pallas_call | solution.py:142
  145.6 7.6 %shard_map.86 = bf16[2,20,720,128]{3,2,1,0:T(8,128)(2,1)} custom-call(s32[22]{0:T(128)S(1)} %and_convert_fusion.valid_ref, bf16[5,720,128]{2,1,0:T(8,128)(2,1)S(1)} %copy.38.next_ref.main_ref, bf16[2,720,128]{2,1,0:T(8,128)(2,1)S(1)} %copy.39.next_ref, f32[2,1,128]{2,1,0:T(1,128)S(1)} %bitcast.24, ...), custom_call_target="tpu_custom_call", output_to_operand_aliasing={{}: (7, {})} | custom-call | tf_op jit(solution)/shard_map/pallas_call | solution.py:142
  (17 shorter events, 0.2 us)
Async XLA Ops:
  0.0 10.6 %copy-start = (f32[720,128]{1,0:T(8,128)S(1)}, f32[720,128]{1,0:T(8,128)}, u32[]{:S(2)}) copy-start(f32[720,128]{1,0:T(8,128)} %param.13) | copy-start | bytes 1105924
  1.7 11.0 %collective-permute-start = (bf16[1,180,256]{2,1,0:T(8,128)(2,1)S(1)}, bf16[1,180,256]{2,1,0:T(8,128)(2,1)S(1)}, u32[]{:S(2)}, u32[]{:S(2)}) collective-permute-start(bf16[1,180,256]{2,1,0:T(8,128)(2,1)S(1)} %copy.44), channel_id=1, source_target_pairs={{0,8},{8,16},{16,24},{24,32},{32,40},{40,48},{48,56},{56,64},{64,7... | collective-permute-start | bytes 276488 | tf_op jit(solution)/shard_map/ppermute | solution.py:21
  5.6 10.0 %collective-permute-start.1 = (bf16[1,180,256]{2,1,0:T(8,128)(2,1)S(1)}, bf16[1,180,256]{2,1,0:T(8,128)(2,1)S(1)}, u32[]{:S(2)}, u32[]{:S(2)}) collective-permute-start(bf16[1,180,256]{2,1,0:T(8,128)(2,1)S(1)} %copy.45), channel_id=1, source_target_pairs={{8,0},{16,8},{24,16},{32,24},{40,32},{48,40},{56,48},{64,56},{72,6... | collective-permute-start | bytes 276488 | tf_op jit(solution)/shard_map/ppermute | solution.py:22
  12.7 6.1 %copy-start.4 = (bf16[3,3,256,256]{3,2,1,0:T(8,128)(2,1)S(1)}, bf16[3,3,256,256]{3,2,1,0:T(8,128)(2,1)}, u32[]{:S(2)}) copy-start(bf16[3,3,256,256]{3,2,1,0:T(8,128)(2,1)} %param.11) | copy-start | bytes 3538948
  15.6 4.2 %copy-start.3 = (bf16[42,180,256]{2,1,0:T(8,128)(2,1)}, bf16[42,180,256]{2,1,0:T(8,128)(2,1)S(1)}, u32[]{:S(2)}) copy-start(bf16[42,180,256]{2,1,0:T(8,128)(2,1)S(1)} %constant_dynamic-update-slice_fusion) | copy-start | bytes 11612164
  15.7 4.7 %collective-permute-start.2 = (bf16[42,1,256]{2,1,0:T(2,128)(2,1)S(1)}, bf16[42,1,256]{2,1,0:T(2,128)(2,1)S(1)}, u32[]{:S(2)}, u32[]{:S(2)}) collective-permute-start(bf16[42,1,256]{2,1,0:T(2,128)(2,1)S(1)} %get-tuple-element.8), channel_id=1, source_target_pairs={{0,1},{1,2},{2,3},{3,4},{4,5},{5,6},{6,7},{7,0},{8,9},{9,10},{10,1... | collective-permute-start | bytes 64520 | tf_op jit(solution)/shard_map/ppermute | solution.py:21
  15.7 4.6 %collective-permute-start.3 = (bf16[42,1,256]{2,1,0:T(2,128)(2,1)S(1)}, bf16[42,1,256]{2,1,0:T(2,128)(2,1)S(1)}, u32[]{:S(2)}, u32[]{:S(2)}) collective-permute-start(bf16[42,1,256]{2,1,0:T(2,128)(2,1)S(1)} %get-tuple-element.9), channel_id=1, source_target_pairs={{1,0},{2,1},{3,2},{4,3},{5,4},{6,5},{7,6},{0,7},{9,8},{10,9},{11,1... | collective-permute-start | bytes 64520 | tf_op jit(solution)/shard_map/ppermute | solution.py:22
  20.1 4.2 %copy-start.2 = (bf16[256,128]{1,0:T(8,128)(2,1)S(1)}, bf16[256,128]{1,0:T(8,128)(2,1)}, u32[]{:S(2)}) copy-start(bf16[256,128]{1,0:T(8,128)(2,1)} %proj_ref.1) | copy-start | bytes 196612
  24.3 18.6 %copy-start.5 = (bf16[3,3,128,128]{3,2,1,0:T(8,128)(2,1)S(1)}, bf16[3,3,128,128]{3,2,1,0:T(8,128)(2,1)}, u32[]{:S(2)}) copy-start(bf16[3,3,128,128]{3,2,1,0:T(8,128)(2,1)} %param.16) | copy-start | bytes 884740
  41.0 8.3 %collective-permute-start.5 = (bf16[1,90,128]{2,1,0:T(8,128)(2,1)S(1)}, bf16[1,90,128]{2,1,0:T(8,128)(2,1)S(1)}, u32[]{:S(2)}, u32[]{:S(2)}) collective-permute-start(bf16[1,90,128]{2,1,0:T(8,128)(2,1)S(1)} %get-tuple-element.16), channel_id=1, source_target_pairs={{0,8},{8,16},{16,24},{24,32},{32,40},{40,48},{48,56},{56,64},{64,7... | collective-permute-start | bytes 69128 | tf_op jit(solution)/shard_map/ppermute | solution.py:21
  43.3 65.5 %collective-permute-start.4 = (bf16[1,90,128]{2,1,0:T(8,128)(2,1)S(1)}, bf16[1,90,128]{2,1,0:T(8,128)(2,1)S(1)}, u32[]{:S(2)}, u32[]{:S(2)}) collective-permute-start(bf16[1,90,128]{2,1,0:T(8,128)(2,1)S(1)} %get-tuple-element.17), channel_id=1, source_target_pairs={{8,0},{16,8},{24,16},{32,24},{40,32},{48,40},{56,48},{64,56},{72,6... | collective-permute-start | bytes 69128 | tf_op jit(solution)/shard_map/ppermute | solution.py:22
  108.4 14.2 %copy-start.1 = (bf16[720,720]{1,0:T(8,128)(2,1)S(1)}, bf16[720,720]{1,0:T(8,128)(2,1)}, u32[]{:S(2)}) copy-start(bf16[720,720]{1,0:T(8,128)(2,1)} %mix_ref.7) | copy-start | bytes 3110404

commit v4 on v2

--- a/solution.py
+++ b/solution.py
@@ -8,7 +8,8 @@
 from jax.sharding import PartitionSpec as P
 
 LEAD_DEV = 2
-HEAD_ROWS = 4
+HEAD_ROWS = 2
+MESH = pl.DeviceIdType.MESH
 
 
 def extended(x, sides, width, wrap):
@@ -94,54 +95,117 @@
     )(padded, w_all, w_proj)
 
 
-def head_kernel(valid_ref, band_ref, scale_ref, shift_ref, w_ref, mix_ref, out_ref):
-    block = pl.program_id(1)
+def head_kernel(tile_ref, scale_ref, shift_ref, w_ref, mix_ref, out_ref, band_ref, mod_ref,
+                hidden_ref, send_sem, recv_sem, local_sem):
+    me = lax.axis_index("lon")
+    n = lax.axis_size("lon")
+    lat = lax.axis_index("lat")
+    last_lat = lax.axis_size("lat") - 1
+    halo_rows, tile_cols, width = tile_ref.shape
     cols = band_ref.shape[1]
-    width = band_ref.shape[2]
-    gain = 1.0 + scale_ref[0]
-    shift = shift_ref[0]
-
-    def modulated(row):
-        value = (band_ref[row].astype(jnp.float32) * gain + shift).astype(jnp.bfloat16)
-        return jnp.where(valid_ref[row] > 0, value, jnp.zeros_like(value))
-
-    def one_row(j, carry):
-        row = block * HEAD_ROWS + j
-        rows = [modulated(row + k) for k in range(3)]
-        stacked = jnp.concatenate(rows, axis=-1)
-        taps = jnp.dot(stacked, w_ref[...], preferred_element_type=jnp.float32)
-        conv = (
-            pltpu.roll(taps[:, :width], 1, 0)
-            + taps[:, width : 2 * width]
-            + pltpu.roll(taps[:, 2 * width :], cols - 1, 0)
+    leads = out_ref.shape[0]
+    step = HEAD_ROWS
+    pieces = halo_rows // step
+
+    barrier = pltpu.get_barrier_semaphore()
+    for s in range(1, n):
+        peer = lax.rem(me + s, n)
+        pl.semaphore_signal(barrier, inc=1, device_id=(lat, peer), device_id_type=MESH)
+    pl.semaphore_wait(barrier, n - 1)
+
+    def slot(piece, source):
+        start = pl.multiple_of(piece * step, step)
+        return band_ref.at[pl.ds(start, step), pl.ds(source * tile_cols, tile_cols)]
+
+    def source_rows(piece):
+        return tile_ref.at[pl.ds(pl.multiple_of(piece * step, step), step)]
+
+    def local_copy(piece):
+        return pltpu.make_async_copy(source_rows(piece), slot(piece, me), local_sem.at[piece])
+
+    def remote_copy(piece, s, target, source):
+        return pltpu.make_async_remote_copy(
+            src_ref=source_rows(piece),
+            dst_ref=slot(piece, source),
+            send_sem=send_sem.at[piece * n + s],
+            recv_sem=recv_sem.at[piece * n + s],
+            device_id=(lat, target),
+            device_id_type=MESH,
         )
-        hidden = jax.nn.gelu(conv).astype(jnp.bfloat16)
-        mixed = jnp.dot(mix_ref[...], hidden, preferred_element_type=jnp.float32)
-        out_ref[0, j] = (rows[1].astype(jnp.float32) + mixed).astype(out_ref.dtype)
+
+    for piece in range(pieces):
+        local_copy(piece).start()
+        for s in range(1, n):
+            remote_copy(piece, s, lax.rem(me + s, n), me).start()
+
+    def arrived(piece):
+        local_copy(piece).wait()
+        for s in range(1, n):
+            remote_copy(piece, s, me, lax.rem(me + n - s, n)).wait_recv()
+
+    arrived(0)
+
+    def one_chunk(k, carry):
+        arrived(k + 1)
+        base = k * step
+        for l in range(leads):
+            gain = 1.0 + scale_ref[l]
+            shift = shift_ref[l]
+            for j in range(step + 2):
+                row = base + j
+                keep = ((row > 0) | (lat > 0)) & ((row < halo_rows - 1) | (lat < last_lat))
+                value = band_ref[row].astype(jnp.float32) * gain + shift
+                value = jnp.where(keep, value, 0.0)
+                mod_ref[l, j] = value.astype(jnp.bfloat16)
+            for j in range(step):
+                stacked = jnp.concatenate([mod_ref[l, j + t] for t in range(3)], axis=-1)
+                taps = jnp.dot(stacked, w_ref[...], preferred_element_type=jnp.float32)
+                conv = (
+                    pltpu.roll(taps[:, :width], 1, 0)
+                    + taps[:, width : 2 * width]
+                    + pltpu.roll(taps[:, 2 * width :], cols - 1, 0)
+                )
+                at = (l * step + j) * width
+                hidden_ref[:, at : at + width] = jax.nn.gelu(conv).astype(jnp.bfloat16)
+        mixed = jnp.dot(mix_ref[...], hidden_ref[...], preferred_element_type=jnp.float32)
+        for l in range(leads):
+            for j in range(step):
+                at = (l * step + j) * width
+                own = mod_ref[l, j + 1].astype(jnp.float32)
+                out_ref[l, base + j] = (own + mixed[:, at : at + width]).astype(out_ref.dtype)
         return carry
 
-    lax.fori_loop(0, HEAD_ROWS, one_row, 0)
-
-
-def head(valid, band, scales, shifts, w_all, zonal_mix):
-    halo_rows, cols, width = band.shape
+    lax.fori_loop(0, pieces - 1, one_chunk, 0)
+
+    for piece in range(pieces):
+        for s in range(1, n):
+            remote_copy(piece, s, lax.rem(me + s, n), me).wait_send()
+
+
+def head(tile, scales, shifts, w_all, zonal_mix, lon_devices):
+    halo_rows, tile_cols, width = tile.shape
     rows = halo_rows - 2
+    cols = tile_cols * lon_devices
     leads = scales.shape[0]
+    pieces = halo_rows // HEAD_ROWS
+    vmem = pl.BlockSpec(memory_space=pltpu.VMEM)
     return pl.pallas_call(
         head_kernel,
         out_shape=jax.ShapeDtypeStruct((leads, rows, cols, width), jnp.bfloat16),
-        grid=(leads, rows // HEAD_ROWS),
-        in_specs=[
-            pl.BlockSpec(memory_space=pltpu.SMEM),
-            pl.BlockSpec((halo_rows, cols, width), lambda l, b: (0, 0, 0)),
-            pl.BlockSpec((1, 1, width), lambda l, b: (l, 0, 0)),
-            pl.BlockSpec((1, 1, width), lambda l, b: (l, 0, 0)),
-            pl.BlockSpec((3 * width, 3 * width), lambda l, b: (0, 0)),
-            pl.BlockSpec((cols, cols), lambda l, b: (0, 0)),
+        in_specs=[pl.BlockSpec(memory_space=pl.ANY), vmem, vmem, vmem, vmem],
+        out_specs=vmem,
+        scratch_shapes=[
+            pltpu.VMEM((halo_rows, cols, width), jnp.bfloat16),
+            pltpu.VMEM((leads, HEAD_ROWS + 2, cols, width), jnp.bfloat16),
+            pltpu.VMEM((cols, leads * HEAD_ROWS * width), jnp.bfloat16),
+            pltpu.SemaphoreType.DMA((pieces * lon_devices,)),
+            pltpu.SemaphoreType.DMA((pieces * lon_devices,)),
+            pltpu.SemaphoreType.DMA((pieces,)),
         ],
-        out_specs=pl.BlockSpec((1, HEAD_ROWS, cols, width), lambda l, b: (l, b, 0, 0)),
-        compiler_params=pltpu.CompilerParams(vmem_limit_bytes=48 * 1024 * 1024),
-    )(valid, band, scales[:, None, :], shifts[:, None, :], w_all, zonal_mix)
+        compiler_params=pltpu.CompilerParams(
+            collective_id=0, has_side_effects=True, vmem_limit_bytes=56 * 1024 * 1024
+        ),
+    )(tile, scales[:, None, :], shifts[:, None, :], w_all, zonal_mix)
 
 
 def shards(inputs, w_enc, w_proj, film_scale, film_shift, lead_ids, w_head, zonal_mix):
@@ -154,16 +218,10 @@
     lon_group = lax.axis_index("lon")
     my_rows = lax.dynamic_slice_in_dim(lead_ids, lon_group * LEAD_DEV, LEAD_DEV)
     tile = extended(tile, (("lat", 0),), 1, False)
-    band = lax.all_gather(tile, "lon", axis=1, tiled=True)
     scales = jnp.take(film_scale, my_rows, axis=0)
     shifts = jnp.take(film_shift, my_rows, axis=0)
-    lat = lax.axis_index("lat")
-    halo_rows = band.shape[0]
-    index = jnp.arange(halo_rows, dtype=jnp.int32)
-    valid = ((index > 0) | (lat > 0)) & ((index < halo_rows - 1) | (lat < lax.axis_size("lat") - 1))
     w_all = jnp.transpose(w_head, (0, 2, 1, 3)).reshape(3 * head_width, 3 * head_width)
-    return head(valid.astype(jnp.int32), band, scales, shifts, w_all, zonal_mix)
-
+    return head(tile, scales, shifts, w_all, zonal_mix, lax.axis_size("lon"))
 
 def solution(mesh):
     in_specs = (P("lat", "lon", None), P(), P(), P(), P(), P(), P(), P())

time: 144 us -> 116 us (0.81)
  waiting for transfers between devices: 34.5 us -> 0.02 us
  between operations: 13.6 us -> 0.22 us
  Pallas kernels: 60.1 us -> 73.1 us
  local copies, waits for them, and re-layouts: 12.2 us -> 18.4 us
  other arithmetic: 2.48 us -> 4.51 us
    all_gather x1 -> x0, waiting for transfers between devices: 31.8 us -> none  [shards(): band = lax.all_gather(tile, 'lon', axis=1, tiled=True)]
    pallas_call x1, Pallas kernels: 43.4 us -> 56.5 us  [head(): pl.pallas_call(head_kernel, out_shape=jax.ShapeDtypeStruct((leads, rows,...]
    unnamed x18 -> x19, local copies, waits for them, and re-layouts: 3.27 us -> 13.3 us
    all_gather x1 -> x0, local copies, waits for them, and re-layouts: 2.78 us -> none  [shards(): band = lax.all_gather(tile, 'lon', axis=1, tiled=True)]
    ppermute x3, waiting for transfers between devices: 1.49 us -> 0.01 us  [extended(): after = lax.ppermute(initial, axis, down)]
  transfers between devices with their start and end apart: 7 -> 6, of which waited for: 4 -> 0; matrix products, arithmetic and copies ran while one was open for 5% -> 8% of each run, Pallas kernels for 0% -> 0%
where the time goes in v4:
time: 116 us; the launch traced here: 115 us
  Pallas kernels  73.1 us (63%)
  starting transfers between devices  19 us (16%)
  local copies, waits for them, and re-layouts  18.4 us (16%)
  other arithmetic  4.51 us (4%)
    pallas_call x1, Pallas kernels, head(): pl.pallas_call(head_kernel, out_shape=jax.ShapeDtypeStruct((leads, rows,...  56.5 us
    pallas_call x1, Pallas kernels, encoder(): pl.pallas_call(encoder_kernel, out_shape=jax.ShapeDtypeStruct((pooled_row...  16.6 us
    unnamed x19, local copies, waits for them, and re-layouts  13.3 us
    ppermute x3, starting transfers between devices, extended(): after = lax.ppermute(initial, axis, down)  12.7 us
    ppermute x3, starting transfers between devices, extended(): before = lax.ppermute(last, axis, up)  6.23 us
    concatenate x2, other arithmetic, extended(): x = jnp.concatenate([before, x, after], axis=dim)  3.1 us
  transfers between devices with their start and end apart: 6, of which 0 were waited for; matrix products, arithmetic and copies ran while one was open for 8% of the time, Pallas kernels for 0%

profile of v4, /device:TPU:24, one launch (start us, length us, event | category | flops | bytes accessed | tf_op | source)
XLA Modules:
  0.0 115.2 jit_solution(14149854045788863939)
XLA Ops:
  0.0 0.0 copy-start
  0.0 1.7 %fusion.6 = (bf16[1,180,256]{2,0,1:T(2,128)(2,1)S(1)}, bf16[1,180,256]{2,0,1:T(2,128)(2,1)S(1)}) fusion(bf16[40,180,256]{2,0,1:T(8,128)(2,1)} %param.10), kind=kLoop, calls=%fused_computation.19 | loop fusion | bytes 368640 | tf_op jit(solution)/shard_map/slice | solution.py:21
  1.7 3.8 %collective-permute-start = (bf16[1,180,256]{2,1,0:T(8,128)(2,1)S(1)}, bf16[1,180,256]{2,1,0:T(8,128)(2,1)S(1)}, u32[]{:S(2)}, u32[]{:S(2)}) collective-permute-start(bf16[1,180,256]{2,1,0:T(8,128)(2,1)S(1)} %copy.23), channel_id=1, source_target_pairs={{0,8},{8,16},{16,24},{24,32},{32,40},{40,48},{48,56},{56,64},{64,7... | collective-permute-start | bytes 276488 | tf_op jit(solution)/shard_map/ppermute | solution.py:22
  5.6 4.2 %collective-permute-start.1 = (bf16[1,180,256]{2,1,0:T(8,128)(2,1)S(1)}, bf16[1,180,256]{2,1,0:T(8,128)(2,1)S(1)}, u32[]{:S(2)}, u32[]{:S(2)}) collective-permute-start(bf16[1,180,256]{2,1,0:T(8,128)(2,1)S(1)} %copy.24), channel_id=1, source_target_pairs={{8,0},{16,8},{24,16},{32,24},{40,32},{48,40},{56,48},{64,56},{72,6... | collective-permute-start | bytes 276488 | tf_op jit(solution)/shard_map/ppermute | solution.py:23
  9.8 0.7 compare_and_fusion
  10.5 0.0 collective-permute-done
  10.6 0.0 copy-start.4
  10.6 2.9 %constant_dynamic-update-slice_fusion.1 = bf16[42,180,256]{2,1,0:T(8,128)(2,1)S(1)} fusion(bf16[42,180,256]{2,1,0:T(8,128)(2,1)S(1)} %constant_dynamic-update-slice_fusion.2, bf16[40,180,256]{2,0,1:T(8,128)(2,1)} %param.10), kind=kLoop, calls=%fused_computation.11 | loop fusion | bytes 7454720
  13.5 0.0 collective-permute-done.1
  13.5 0.0 copy-start.2
  13.5 1.9 %copy-done.2 = bf16[42,180,256]{2,1,0:T(8,128)(2,1)} copy-done((bf16[42,180,256]{2,1,0:T(8,128)(2,1)}, bf16[42,180,256]{2,1,0:T(8,128)(2,1)S(1)}, u32[]{:S(2)}) %copy-start.2) | copy-done | bytes 3870744
  15.4 0.1 fusion.5
  15.5 0.0 collective-permute-start.2
  15.5 2.9 %collective-permute-start.3 = (bf16[42,1,256]{2,1,0:T(2,128)(2,1)S(1)}, bf16[42,1,256]{2,1,0:T(2,128)(2,1)S(1)}, u32[]{:S(2)}, u32[]{:S(2)}) collective-permute-start(bf16[42,1,256]{2,1,0:T(2,128)(2,1)S(1)} %get-tuple-element.9), channel_id=1, source_target_pairs={{1,0},{2,1},{3,2},{4,3},{5,4},{6,5},{7,6},{0,7},{9,8},{10,9},{11,1... | collective-permute-start | bytes 64520 | tf_op jit(solution)/shard_map/ppermute | solution.py:23
  18.5 0.0 copy-done
  18.5 0.6 gather_fusion.1
  19.0 1.5 %gather_fusion = f32[2,128]{1,0:T(2,128)S(1)} fusion(f32[720,128]{1,0:T(8,128)} %param.13, s32[1024]{0:T(1024)S(1)} %pad_clamp_fusion), kind=kCustom, calls=%fused_computation.clone | custom fusion | bytes 2056 | tf_op jit(solution)/shard_map/jit(_take)/gather | solution.py:221
  20.6 0.0 copy-start.3
  20.6 0.0 copy-done.4
  20.6 1.0 copy.17
  21.6 0.3 copy.19
  21.9 0.0 copy-start.1
  21.9 0.0 collective-permute-done.2
  21.9 0.0 collective-permute-done.3
  21.9 0.8 copy-done.3
  22.7 2.2 %fusion.4.x_ref = bf16[42,184,256]{2,1,0:T(8,128)(2,1)S(1)} fusion(bf16[42,1,256]{2,1,0:T(2,128)(2,1)S(1)} %collective-permute-done.3, bf16[42,180,256]{2,1,0:T(8,128)(2,1)S(1)} %copy-done.3, bf16[42,1,256]{2,1,0:T(2,128)(2,1)S(1)} %collective-permute-done.2), kind=kLoop, calls=%fused_computation.7 | loop fusion | flops 19783680 | bytes 7870464 | tf_op jit(solution)/shard_map/concatenate | solution.py:24
  24.9 0.0 copy-start.5
  24.9 0.0 copy-done.1
  25.0 16.6 %shard_map.82 = bf16[20,90,128]{2,1,0:T(8,128)(2,1)S(1)} custom-call(bf16[42,184,256]{2,1,0:T(8,128)(2,1)S(1)} %fusion.4.x_ref, bf16[768,768]{1,0:T(8,128)(2,1)S(1)} %bitcast.12, bf16[256,128]{1,0:T(8,128)(2,1)S(1)} %copy-done.1), custom_call_target="tpu_custom_call" | custom-call | tf_op jit(solution)/shard_map/pallas_call | solution.py:88
  41.6 2.4 %collective-permute-start.4 = (bf16[1,90,128]{2,1,0:T(8,128)(2,1)S(1)}, bf16[1,90,128]{2,1,0:T(8,128)(2,1)S(1)}, u32[]{:S(2)}, u32[]{:S(2)}) collective-permute-start(bf16[1,90,128]{2,1,0:T(8,128)(2,1)S(1)} %get-tuple-element.12), channel_id=1, source_target_pairs={{0,8},{8,16},{16,24},{24,32},{32,40},{40,48},{48,56},{56,64},{64,7... | collective-permute-start | bytes 69128 | tf_op jit(solution)/shard_map/ppermute | solution.py:22
  44.0 5.6 %collective-permute-start.5 = (bf16[1,90,128]{2,1,0:T(8,128)(2,1)S(1)}, bf16[1,90,128]{2,1,0:T(8,128)(2,1)S(1)}, u32[]{:S(2)}, u32[]{:S(2)}) collective-permute-start(bf16[1,90,128]{2,1,0:T(8,128)(2,1)S(1)} %get-tuple-element.13), channel_id=1, source_target_pairs={{8,0},{16,8},{24,16},{32,24},{40,32},{48,40},{56,48},{64,56},{72,6... | collective-permute-start | bytes 69128 | tf_op jit(solution)/shard_map/ppermute | solution.py:23
  49.6 0.7 broadcast_select_fusion
  50.2 0.0 copy-done.5
  50.2 0.3 copy.18
  50.5 0.8 copy.25
  51.3 0.0 collective-permute-done.4
  51.3 0.0 collective-permute-done.5
  51.3 0.9 pad_maximum_fusion.tile_ref
  52.1 56.5 %shard_map.83 = bf16[2,20,720,128]{3,2,1,0:T(8,128)(2,1)} custom-call(bf16[22,90,128]{2,1,0:T(8,128)(2,1)} %pad_maximum_fusion.tile_ref, f32[2,1,128]{2,1,0:T(1,128)} %bitcast.19, f32[2,1,128]{2,1,0:T(1,128)} %bitcast.18, bf16[384,384]{1,0:T(8,128)(2,1)} %bitcast.15, bf16[720,720]{1,0:T(8,128)(2,1)} %mix_ref.1), custom_call_target="tpu_custom_call" | custom-call | tf_op jit(solution)/shard_map/pallas_call | solution.py:192
  108.6 6.6 %copy.29 = bf16[2,20,720,128]{3,2,1,0:T(8,128)(2,1)} copy(bf16[2,20,720,128]{3,2,1,0:T(8,128)(2,1)} %shard_map.83) | data formatting | bytes 14745600
  (6 shorter events, 0.1 us)
Async XLA Ops:
  0.0 18.5 %copy-start = (f32[720,128]{1,0:T(8,128)S(1)}, f32[720,128]{1,0:T(8,128)}, u32[]{:S(2)}) copy-start(f32[720,128]{1,0:T(8,128)} %param.14) | copy-start | bytes 1105924
  1.7 8.8 %collective-permute-start = (bf16[1,180,256]{2,1,0:T(8,128)(2,1)S(1)}, bf16[1,180,256]{2,1,0:T(8,128)(2,1)S(1)}, u32[]{:S(2)}, u32[]{:S(2)}) collective-permute-start(bf16[1,180,256]{2,1,0:T(8,128)(2,1)S(1)} %copy.23), channel_id=1, source_target_pairs={{0,8},{8,16},{16,24},{24,32},{32,40},{40,48},{48,56},{56,64},{64,7... | collective-permute-start | bytes 276488 | tf_op jit(solution)/shard_map/ppermute | solution.py:22
  5.6 7.9 %collective-permute-start.1 = (bf16[1,180,256]{2,1,0:T(8,128)(2,1)S(1)}, bf16[1,180,256]{2,1,0:T(8,128)(2,1)S(1)}, u32[]{:S(2)}, u32[]{:S(2)}) collective-permute-start(bf16[1,180,256]{2,1,0:T(8,128)(2,1)S(1)} %copy.24), channel_id=1, source_target_pairs={{8,0},{16,8},{24,16},{32,24},{40,32},{48,40},{56,48},{64,56},{72,6... | collective-permute-start | bytes 276488 | tf_op jit(solution)/shard_map/ppermute | solution.py:23
  10.6 10.0 %copy-start.4 = (bf16[3,3,256,256]{3,2,1,0:T(8,128)(2,1)S(1)}, bf16[3,3,256,256]{3,2,1,0:T(8,128)(2,1)}, u32[]{:S(2)}) copy-start(bf16[3,3,256,256]{3,2,1,0:T(8,128)(2,1)} %param.11) | copy-start | bytes 3538948
  13.5 1.9 %copy-start.2 = (bf16[42,180,256]{2,1,0:T(8,128)(2,1)}, bf16[42,180,256]{2,1,0:T(8,128)(2,1)S(1)}, u32[]{:S(2)}) copy-start(bf16[42,180,256]{2,1,0:T(8,128)(2,1)S(1)} %constant_dynamic-update-slice_fusion) | copy-start | bytes 11612164
  15.5 6.4 %collective-permute-start.2 = (bf16[42,1,256]{2,1,0:T(2,128)(2,1)S(1)}, bf16[42,1,256]{2,1,0:T(2,128)(2,1)S(1)}, u32[]{:S(2)}, u32[]{:S(2)}) collective-permute-start(bf16[42,1,256]{2,1,0:T(2,128)(2,1)S(1)} %get-tuple-element.8), channel_id=1, source_target_pairs={{0,1},{1,2},{2,3},{3,4},{4,5},{5,6},{6,7},{7,0},{8,9},{9,10},{10,1... | collective-permute-start | bytes 64520 | tf_op jit(solution)/shard_map/ppermute | solution.py:22
  15.5 6.4 %collective-permute-start.3 = (bf16[42,1,256]{2,1,0:T(2,128)(2,1)S(1)}, bf16[42,1,256]{2,1,0:T(2,128)(2,1)S(1)}, u32[]{:S(2)}, u32[]{:S(2)}) collective-permute-start(bf16[42,1,256]{2,1,0:T(2,128)(2,1)S(1)} %get-tuple-element.9), channel_id=1, source_target_pairs={{1,0},{2,1},{3,2},{4,3},{5,4},{6,5},{7,6},{0,7},{9,8},{10,9},{11,1... | collective-permute-start | bytes 64520 | tf_op jit(solution)/shard_map/ppermute | solution.py:23
  20.6 2.1 %copy-start.3 = (bf16[42,180,256]{2,1,0:T(8,128)(2,1)S(1)}, bf16[42,180,256]{2,1,0:T(8,128)(2,1)}, u32[]{:S(2)}) copy-start(bf16[42,180,256]{2,1,0:T(8,128)(2,1)} %copy-done.2) | copy-start | bytes 11612164
  21.9 3.0 %copy-start.1 = (bf16[256,128]{1,0:T(8,128)(2,1)S(1)}, bf16[256,128]{1,0:T(8,128)(2,1)}, u32[]{:S(2)}) copy-start(bf16[256,128]{1,0:T(8,128)(2,1)} %proj_ref.1) | copy-start | bytes 196612
  24.9 25.3 %copy-start.5 = (bf16[3,3,128,128]{3,2,1,0:T(8,128)(2,1)S(1)}, bf16[3,3,128,128]{3,2,1,0:T(8,128)(2,1)}, u32[]{:S(2)}) copy-start(bf16[3,3,128,128]{3,2,1,0:T(8,128)(2,1)} %param.16) | copy-start | bytes 884740
  41.6 9.7 %collective-permute-start.4 = (bf16[1,90,128]{2,1,0:T(8,128)(2,1)S(1)}, bf16[1,90,128]{2,1,0:T(8,128)(2,1)S(1)}, u32[]{:S(2)}, u32[]{:S(2)}) collective-permute-start(bf16[1,90,128]{2,1,0:T(8,128)(2,1)S(1)} %get-tuple-element.12), channel_id=1, source_target_pairs={{0,8},{8,16},{16,24},{24,32},{32,40},{40,48},{48,56},{56,64},{64,7... | collective-permute-start | bytes 69128 | tf_op jit(solution)/shard_map/ppermute | solution.py:22
  44.0 7.3 %collective-permute-start.5 = (bf16[1,90,128]{2,1,0:T(8,128)(2,1)S(1)}, bf16[1,90,128]{2,1,0:T(8,128)(2,1)S(1)}, u32[]{:S(2)}, u32[]{:S(2)}) collective-permute-start(bf16[1,90,128]{2,1,0:T(8,128)(2,1)S(1)} %get-tuple-element.13), channel_id=1, source_target_pairs={{8,0},{16,8},{24,16},{32,24},{40,32},{48,40},{56,48},{64,56},{72,6... | collective-permute-start | bytes 69128 | tf_op jit(solution)/shard_map/ppermute | solution.py:23

commit v5 on v4

--- a/solution.py
+++ b/solution.py
@@ -107,11 +107,26 @@
     step = HEAD_ROWS
     pieces = halo_rows // step
 
+    chips = n // 2
+    chip = me // 2
+    core = me % 2
+    sense = 1 - 2 * core
+    kinds = 7
+
+    def device(at_chip, at_core):
+        return 2 * lax.rem(at_chip + 2 * chips, chips) + at_core
+
+    sibling = device(chip, 1 - core)
+    east = device(chip + 1, core)
+    west = device(chip - 1, core)
+    far = device(chip + 2, core)
+    behind = device(chip - sense, core)
+    ahead = device(chip + sense, core)
+
     barrier = pltpu.get_barrier_semaphore()
-    for s in range(1, n):
-        peer = lax.rem(me + s, n)
+    for peer in (sibling, east, west):
         pl.semaphore_signal(barrier, inc=1, device_id=(lat, peer), device_id_type=MESH)
-    pl.semaphore_wait(barrier, n - 1)
+    pl.semaphore_wait(barrier, 3)
 
     def slot(piece, source):
         start = pl.multiple_of(piece * step, step)
@@ -123,29 +138,67 @@
     def local_copy(piece):
         return pltpu.make_async_copy(source_rows(piece), slot(piece, me), local_sem.at[piece])
 
-    def remote_copy(piece, s, target, source):
+    def transfer(piece, kind, origin, target, own=False):
         return pltpu.make_async_remote_copy(
-            src_ref=source_rows(piece),
-            dst_ref=slot(piece, source),
-            send_sem=send_sem.at[piece * n + s],
-            recv_sem=recv_sem.at[piece * n + s],
+            src_ref=source_rows(piece) if own else slot(piece, origin),
+            dst_ref=slot(piece, origin),
+            send_sem=send_sem.at[piece * kinds + kind],
+            recv_sem=recv_sem.at[piece * kinds + kind],
             device_id=(lat, target),
             device_id_type=MESH,
         )
 
+    def sends(piece):
+        return [
+            transfer(piece, 0, me, sibling, own=True),
+            transfer(piece, 1, me, east, own=True),
+            transfer(piece, 2, me, west, own=True),
+            transfer(piece, 3, behind, ahead),
+            transfer(piece, 4, west, sibling),
+            transfer(piece, 5, east, sibling),
+            transfer(piece, 6, far, sibling),
+        ]
+
+    def receive(piece, kind, origin):
+        transfer(piece, kind, origin, me).wait_recv()
+
     for piece in range(pieces):
         local_copy(piece).start()
-        for s in range(1, n):
-            remote_copy(piece, s, lax.rem(me + s, n), me).start()
+        for copy in sends(piece)[:3]:
+            copy.start()
+
+    def forward_x(piece):
+        receive(piece, 1 + core, behind)
+        sends(piece)[3].start()
+
+    def forward_sibling(piece):
+        receive(piece, 2 - core, ahead)
+        receive(piece, 3, far)
+        for copy in sends(piece)[4:]:
+            copy.start()
 
     def arrived(piece):
         local_copy(piece).wait()
-        for s in range(1, n):
-            remote_copy(piece, s, me, lax.rem(me + n - s, n)).wait_recv()
-
+        receive(piece, 0, sibling)
+        receive(piece, 4, device(chip - 1, 1 - core))
+        receive(piece, 5, device(chip + 1, 1 - core))
+        receive(piece, 6, device(chip + 2, 1 - core))
+
+    for piece in range(min(3, pieces)):
+        forward_x(piece)
+    for piece in range(min(2, pieces)):
+        forward_sibling(piece)
     arrived(0)
 
     def one_chunk(k, carry):
+        @pl.when(k + 3 < pieces)
+        def _():
+            forward_x(k + 3)
+
+        @pl.when(k + 2 < pieces)
+        def _():
+            forward_sibling(k + 2)
+
         arrived(k + 1)
         base = k * step
         for l in range(leads):
@@ -178,8 +231,8 @@
     lax.fori_loop(0, pieces - 1, one_chunk, 0)
 
     for piece in range(pieces):
-        for s in range(1, n):
-            remote_copy(piece, s, lax.rem(me + s, n), me).wait_send()
+        for copy in sends(piece):
+            copy.wait_send()
 
 
 def head(tile, scales, shifts, w_all, zonal_mix, lon_devices):
@@ -198,8 +251,8 @@
             pltpu.VMEM((halo_rows, cols, width), jnp.bfloat16),
             pltpu.VMEM((leads, HEAD_ROWS + 2, cols, width), jnp.bfloat16),
             pltpu.VMEM((cols, leads * HEAD_ROWS * width), jnp.bfloat16),
-            pltpu.SemaphoreType.DMA((pieces * lon_devices,)),
-            pltpu.SemaphoreType.DMA((pieces * lon_devices,)),
+            pltpu.SemaphoreType.DMA((pieces * 7,)),
+            pltpu.SemaphoreType.DMA((pieces * 7,)),
             pltpu.SemaphoreType.DMA((pieces,)),
         ],
         compiler_params=pltpu.CompilerParams(

time: 116 us -> 109 us (0.940)
  Pallas kernels: 73.1 us -> 66.6 us
    pallas_call x1, Pallas kernels: 56.5 us -> 49.9 us  [head(): pl.pallas_call(head_kernel, out_shape=jax.ShapeDtypeStruct((leads, rows,...]
where the time goes in v5:
time: 109 us
  Pallas kernels  66.6 us (61%)
  starting transfers between devices  19 us (17%)
  local copies, waits for them, and re-layouts  18.4 us (17%)
  other arithmetic  4.51 us (4%)
    pallas_call x1, Pallas kernels, head(): pl.pallas_call(head_kernel, out_shape=jax.ShapeDtypeStruct((leads, rows,...  49.9 us
    pallas_call x1, Pallas kernels, encoder(): pl.pallas_call(encoder_kernel, out_shape=jax.ShapeDtypeStruct((pooled_row...  16.6 us
    unnamed x19, local copies, waits for them, and re-layouts  13.3 us
    ppermute x3, starting transfers between devices, extended(): after = lax.ppermute(initial, axis, down)  12.7 us
    ppermute x3, starting transfers between devices, extended(): before = lax.ppermute(last, axis, up)  6.23 us
    concatenate x2, other arithmetic, extended(): x = jnp.concatenate([before, x, after], axis=dim)  3.1 us
  transfers between devices with their start and end apart: 6, of which 0 were waited for; matrix products, arithmetic and copies ran while one was open for 8% of the time, Pallas kernels for 0%

profile of v5, /device:TPU:24, one launch (start us, length us, event | category | flops | bytes accessed | tf_op | source)
XLA Modules:
  0.0 108.7 jit_solution(13836999293545043719)
XLA Ops:
  0.0 0.0 copy-start
  0.0 1.7 %fusion.6 = (bf16[1,180,256]{2,0,1:T(2,128)(2,1)S(1)}, bf16[1,180,256]{2,0,1:T(2,128)(2,1)S(1)}) fusion(bf16[40,180,256]{2,0,1:T(8,128)(2,1)} %param.10), kind=kLoop, calls=%fused_computation.19 | loop fusion | bytes 368640 | tf_op jit(solution)/shard_map/slice | solution.py:21
  1.7 3.8 %collective-permute-start = (bf16[1,180,256]{2,1,0:T(8,128)(2,1)S(1)}, bf16[1,180,256]{2,1,0:T(8,128)(2,1)S(1)}, u32[]{:S(2)}, u32[]{:S(2)}) collective-permute-start(bf16[1,180,256]{2,1,0:T(8,128)(2,1)S(1)} %copy.23), channel_id=1, source_target_pairs={{0,8},{8,16},{16,24},{24,32},{32,40},{40,48},{48,56},{56,64},{64,7... | collective-permute-start | bytes 276488 | tf_op jit(solution)/shard_map/ppermute | solution.py:22
  5.6 4.2 %collective-permute-start.1 = (bf16[1,180,256]{2,1,0:T(8,128)(2,1)S(1)}, bf16[1,180,256]{2,1,0:T(8,128)(2,1)S(1)}, u32[]{:S(2)}, u32[]{:S(2)}) collective-permute-start(bf16[1,180,256]{2,1,0:T(8,128)(2,1)S(1)} %copy.24), channel_id=1, source_target_pairs={{8,0},{16,8},{24,16},{32,24},{40,32},{48,40},{56,48},{64,56},{72,6... | collective-permute-start | bytes 276488 | tf_op jit(solution)/shard_map/ppermute | solution.py:23
  9.8 0.7 compare_and_fusion
  10.5 0.0 collective-permute-done
  10.6 0.0 copy-start.4
  10.6 2.9 %constant_dynamic-update-slice_fusion.1 = bf16[42,180,256]{2,1,0:T(8,128)(2,1)S(1)} fusion(bf16[42,180,256]{2,1,0:T(8,128)(2,1)S(1)} %constant_dynamic-update-slice_fusion.2, bf16[40,180,256]{2,0,1:T(8,128)(2,1)} %param.10), kind=kLoop, calls=%fused_computation.11 | loop fusion | bytes 7454720
  13.5 0.0 collective-permute-done.1
  13.5 0.0 copy-start.2
  13.5 1.9 %copy-done.2 = bf16[42,180,256]{2,1,0:T(8,128)(2,1)} copy-done((bf16[42,180,256]{2,1,0:T(8,128)(2,1)}, bf16[42,180,256]{2,1,0:T(8,128)(2,1)S(1)}, u32[]{:S(2)}) %copy-start.2) | copy-done | bytes 3870744
  15.4 0.1 fusion.5
  15.5 0.0 collective-permute-start.2
  15.5 2.9 %collective-permute-start.3 = (bf16[42,1,256]{2,1,0:T(2,128)(2,1)S(1)}, bf16[42,1,256]{2,1,0:T(2,128)(2,1)S(1)}, u32[]{:S(2)}, u32[]{:S(2)}) collective-permute-start(bf16[42,1,256]{2,1,0:T(2,128)(2,1)S(1)} %get-tuple-element.9), channel_id=1, source_target_pairs={{1,0},{2,1},{3,2},{4,3},{5,4},{6,5},{7,6},{0,7},{9,8},{10,9},{11,1... | collective-permute-start | bytes 64520 | tf_op jit(solution)/shard_map/ppermute | solution.py:23
  18.5 0.0 copy-done
  18.5 0.6 gather_fusion.1
  19.0 1.5 %gather_fusion = f32[2,128]{1,0:T(2,128)S(1)} fusion(f32[720,128]{1,0:T(8,128)} %param.13, s32[1024]{0:T(1024)S(1)} %pad_clamp_fusion), kind=kCustom, calls=%fused_computation.clone | custom fusion | bytes 2056 | tf_op jit(solution)/shard_map/jit(_take)/gather | solution.py:274
  20.6 0.0 copy-start.3
  20.6 0.0 copy-done.4
  20.6 1.0 copy.17
  21.6 0.3 copy.19
  21.9 0.0 copy-start.1
  21.9 0.0 collective-permute-done.2
  21.9 0.0 collective-permute-done.3
  21.9 0.8 copy-done.3
  22.7 2.2 %fusion.4.x_ref = bf16[42,184,256]{2,1,0:T(8,128)(2,1)S(1)} fusion(bf16[42,1,256]{2,1,0:T(2,128)(2,1)S(1)} %collective-permute-done.3, bf16[42,180,256]{2,1,0:T(8,128)(2,1)S(1)} %copy-done.3, bf16[42,1,256]{2,1,0:T(2,128)(2,1)S(1)} %collective-permute-done.2), kind=kLoop, calls=%fused_computation.7 | loop fusion | flops 19783680 | bytes 7870464 | tf_op jit(solution)/shard_map/concatenate | solution.py:24
  24.9 0.0 copy-start.5
  24.9 0.0 copy-done.1
  25.0 16.6 %shard_map.82 = bf16[20,90,128]{2,1,0:T(8,128)(2,1)S(1)} custom-call(bf16[42,184,256]{2,1,0:T(8,128)(2,1)S(1)} %fusion.4.x_ref, bf16[768,768]{1,0:T(8,128)(2,1)S(1)} %bitcast.12, bf16[256,128]{1,0:T(8,128)(2,1)S(1)} %copy-done.1), custom_call_target="tpu_custom_call" | custom-call | tf_op jit(solution)/shard_map/pallas_call | solution.py:88
  41.6 2.4 %collective-permute-start.4 = (bf16[1,90,128]{2,1,0:T(8,128)(2,1)S(1)}, bf16[1,90,128]{2,1,0:T(8,128)(2,1)S(1)}, u32[]{:S(2)}, u32[]{:S(2)}) collective-permute-start(bf16[1,90,128]{2,1,0:T(8,128)(2,1)S(1)} %get-tuple-element.12), channel_id=1, source_target_pairs={{0,8},{8,16},{16,24},{24,32},{32,40},{40,48},{48,56},{56,64},{64,7... | collective-permute-start | bytes 69128 | tf_op jit(solution)/shard_map/ppermute | solution.py:22
  44.0 5.6 %collective-permute-start.5 = (bf16[1,90,128]{2,1,0:T(8,128)(2,1)S(1)}, bf16[1,90,128]{2,1,0:T(8,128)(2,1)S(1)}, u32[]{:S(2)}, u32[]{:S(2)}) collective-permute-start(bf16[1,90,128]{2,1,0:T(8,128)(2,1)S(1)} %get-tuple-element.13), channel_id=1, source_target_pairs={{8,0},{16,8},{24,16},{32,24},{40,32},{48,40},{56,48},{64,56},{72,6... | collective-permute-start | bytes 69128 | tf_op jit(solution)/shard_map/ppermute | solution.py:23
  49.6 0.7 broadcast_select_fusion
  50.2 0.0 copy-done.5
  50.2 0.3 copy.18
  50.5 0.8 copy.25
  51.3 0.0 collective-permute-done.4
  51.3 0.0 collective-permute-done.5
  51.3 0.9 pad_maximum_fusion.tile_ref
  52.1 49.9 %shard_map.83 = bf16[2,20,720,128]{3,2,1,0:T(8,128)(2,1)} custom-call(bf16[22,90,128]{2,1,0:T(8,128)(2,1)} %pad_maximum_fusion.tile_ref, f32[2,1,128]{2,1,0:T(1,128)} %bitcast.19, f32[2,1,128]{2,1,0:T(1,128)} %bitcast.18, bf16[384,384]{1,0:T(8,128)(2,1)} %bitcast.15, bf16[720,720]{1,0:T(8,128)(2,1)} %mix_ref.1), custom_call_target="tpu_custom_call" | custom-call | tf_op jit(solution)/shard_map/pallas_call | solution.py:245
  102.1 6.6 %copy.29 = bf16[2,20,720,128]{3,2,1,0:T(8,128)(2,1)} copy(bf16[2,20,720,128]{3,2,1,0:T(8,128)(2,1)} %shard_map.83) | data formatting | bytes 14745600
  (6 shorter events, 0.1 us)
Async XLA Ops:
  0.0 18.5 %copy-start = (f32[720,128]{1,0:T(8,128)S(1)}, f32[720,128]{1,0:T(8,128)}, u32[]{:S(2)}) copy-start(f32[720,128]{1,0:T(8,128)} %param.14) | copy-start | bytes 1105924
  1.7 8.8 %collective-permute-start = (bf16[1,180,256]{2,1,0:T(8,128)(2,1)S(1)}, bf16[1,180,256]{2,1,0:T(8,128)(2,1)S(1)}, u32[]{:S(2)}, u32[]{:S(2)}) collective-permute-start(bf16[1,180,256]{2,1,0:T(8,128)(2,1)S(1)} %copy.23), channel_id=1, source_target_pairs={{0,8},{8,16},{16,24},{24,32},{32,40},{40,48},{48,56},{56,64},{64,7... | collective-permute-start | bytes 276488 | tf_op jit(solution)/shard_map/ppermute | solution.py:22
  5.6 7.9 %collective-permute-start.1 = (bf16[1,180,256]{2,1,0:T(8,128)(2,1)S(1)}, bf16[1,180,256]{2,1,0:T(8,128)(2,1)S(1)}, u32[]{:S(2)}, u32[]{:S(2)}) collective-permute-start(bf16[1,180,256]{2,1,0:T(8,128)(2,1)S(1)} %copy.24), channel_id=1, source_target_pairs={{8,0},{16,8},{24,16},{32,24},{40,32},{48,40},{56,48},{64,56},{72,6... | collective-permute-start | bytes 276488 | tf_op jit(solution)/shard_map/ppermute | solution.py:23
  10.6 10.0 %copy-start.4 = (bf16[3,3,256,256]{3,2,1,0:T(8,128)(2,1)S(1)}, bf16[3,3,256,256]{3,2,1,0:T(8,128)(2,1)}, u32[]{:S(2)}) copy-start(bf16[3,3,256,256]{3,2,1,0:T(8,128)(2,1)} %param.11) | copy-start | bytes 3538948
  13.5 1.9 %copy-start.2 = (bf16[42,180,256]{2,1,0:T(8,128)(2,1)}, bf16[42,180,256]{2,1,0:T(8,128)(2,1)S(1)}, u32[]{:S(2)}) copy-start(bf16[42,180,256]{2,1,0:T(8,128)(2,1)S(1)} %constant_dynamic-update-slice_fusion) | copy-start | bytes 11612164
  15.5 6.4 %collective-permute-start.2 = (bf16[42,1,256]{2,1,0:T(2,128)(2,1)S(1)}, bf16[42,1,256]{2,1,0:T(2,128)(2,1)S(1)}, u32[]{:S(2)}, u32[]{:S(2)}) collective-permute-start(bf16[42,1,256]{2,1,0:T(2,128)(2,1)S(1)} %get-tuple-element.8), channel_id=1, source_target_pairs={{0,1},{1,2},{2,3},{3,4},{4,5},{5,6},{6,7},{7,0},{8,9},{9,10},{10,1... | collective-permute-start | bytes 64520 | tf_op jit(solution)/shard_map/ppermute | solution.py:22
  15.5 6.4 %collective-permute-start.3 = (bf16[42,1,256]{2,1,0:T(2,128)(2,1)S(1)}, bf16[42,1,256]{2,1,0:T(2,128)(2,1)S(1)}, u32[]{:S(2)}, u32[]{:S(2)}) collective-permute-start(bf16[42,1,256]{2,1,0:T(2,128)(2,1)S(1)} %get-tuple-element.9), channel_id=1, source_target_pairs={{1,0},{2,1},{3,2},{4,3},{5,4},{6,5},{7,6},{0,7},{9,8},{10,9},{11,1... | collective-permute-start | bytes 64520 | tf_op jit(solution)/shard_map/ppermute | solution.py:23
  20.6 2.1 %copy-start.3 = (bf16[42,180,256]{2,1,0:T(8,128)(2,1)S(1)}, bf16[42,180,256]{2,1,0:T(8,128)(2,1)}, u32[]{:S(2)}) copy-start(bf16[42,180,256]{2,1,0:T(8,128)(2,1)} %copy-done.2) | copy-start | bytes 11612164
  21.9 3.0 %copy-start.1 = (bf16[256,128]{1,0:T(8,128)(2,1)S(1)}, bf16[256,128]{1,0:T(8,128)(2,1)}, u32[]{:S(2)}) copy-start(bf16[256,128]{1,0:T(8,128)(2,1)} %proj_ref.1) | copy-start | bytes 196612
  24.9 25.3 %copy-start.5 = (bf16[3,3,128,128]{3,2,1,0:T(8,128)(2,1)S(1)}, bf16[3,3,128,128]{3,2,1,0:T(8,128)(2,1)}, u32[]{:S(2)}) copy-start(bf16[3,3,128,128]{3,2,1,0:T(8,128)(2,1)} %param.16) | copy-start | bytes 884740
  41.6 9.7 %collective-permute-start.4 = (bf16[1,90,128]{2,1,0:T(8,128)(2,1)S(1)}, bf16[1,90,128]{2,1,0:T(8,128)(2,1)S(1)}, u32[]{:S(2)}, u32[]{:S(2)}) collective-permute-start(bf16[1,90,128]{2,1,0:T(8,128)(2,1)S(1)} %get-tuple-element.12), channel_id=1, source_target_pairs={{0,8},{8,16},{16,24},{24,32},{32,40},{40,48},{48,56},{56,64},{64,7... | collective-permute-start | bytes 69128 | tf_op jit(solution)/shard_map/ppermute | solution.py:22
  44.0 7.3 %collective-permute-start.5 = (bf16[1,90,128]{2,1,0:T(8,128)(2,1)S(1)}, bf16[1,90,128]{2,1,0:T(8,128)(2,1)S(1)}, u32[]{:S(2)}, u32[]{:S(2)}) collective-permute-start(bf16[1,90,128]{2,1,0:T(8,128)(2,1)S(1)} %get-tuple-element.13), channel_id=1, source_target_pairs={{8,0},{16,8},{24,16},{32,24},{40,32},{48,40},{56,48},{64,56},{72,6... | collective-permute-start | bytes 69128 | tf_op jit(solution)/shard_map/ppermute | solution.py:23

commit v6 on v5

--- a/solution.py
+++ b/solution.py
@@ -9,6 +9,7 @@
 
 LEAD_DEV = 2
 HEAD_ROWS = 2
+AHEAD = 1
 MESH = pl.DeviceIdType.MESH
 
 
@@ -162,7 +163,7 @@
     def receive(piece, kind, origin):
         transfer(piece, kind, origin, me).wait_recv()
 
-    for piece in range(pieces):
+    def direct(piece):
         local_copy(piece).start()
         for copy in sends(piece)[:3]:
             copy.start()
@@ -184,6 +185,8 @@
         receive(piece, 5, device(chip + 1, 1 - core))
         receive(piece, 6, device(chip + 2, 1 - core))
 
+    for piece in range(min(AHEAD + 3, pieces)):
+        direct(piece)
     for piece in range(min(3, pieces)):
         forward_x(piece)
     for piece in range(min(2, pieces)):
@@ -191,6 +194,10 @@
     arrived(0)
 
     def one_chunk(k, carry):
+        @pl.when(k + AHEAD + 3 < pieces)
+        def _():
+            direct(k + AHEAD + 3)
+
         @pl.when(k + 3 < pieces)
         def _():
             forward_x(k + 3)

time: 109 us -> 106 us (0.972)
  Pallas kernels: 66.6 us -> 63.7 us
    pallas_call x1, Pallas kernels: 49.9 us -> 47 us  [head(): pl.pallas_call(head_kernel, out_shape=jax.ShapeDtypeStruct((leads, rows,...]
where the time goes in v6:
time: 106 us
  Pallas kernels  63.7 us (60%)
  starting transfers between devices  19 us (18%)
  local copies, waits for them, and re-layouts  18.4 us (17%)
  other arithmetic  4.51 us (4%)
    pallas_call x1, Pallas kernels, head(): pl.pallas_call(head_kernel, out_shape=jax.ShapeDtypeStruct((leads, rows,...  47 us
    pallas_call x1, Pallas kernels, encoder(): pl.pallas_call(encoder_kernel, out_shape=jax.ShapeDtypeStruct((pooled_row...  16.6 us
    unnamed x19, local copies, waits for them, and re-layouts  13.3 us
    ppermute x3, starting transfers between devices, extended(): after = lax.ppermute(initial, axis, down)  12.7 us
    ppermute x3, starting transfers between devices, extended(): before = lax.ppermute(last, axis, up)  6.23 us
    concatenate x2, other arithmetic, extended(): x = jnp.concatenate([before, x, after], axis=dim)  3.1 us
  transfers between devices with their start and end apart: 6, of which 0 were waited for; matrix products, arithmetic and copies ran while one was open for 8% of the time, Pallas kernels for 0%

profile of v6, /device:TPU:24, one launch (start us, length us, event | category | flops | bytes accessed | tf_op | source)
XLA Modules:
  0.0 105.8 jit_solution(11888456824259644265)
XLA Ops:
  0.0 0.0 copy-start
  0.0 1.7 %fusion.6 = (bf16[1,180,256]{2,0,1:T(2,128)(2,1)S(1)}, bf16[1,180,256]{2,0,1:T(2,128)(2,1)S(1)}) fusion(bf16[40,180,256]{2,0,1:T(8,128)(2,1)} %param.10), kind=kLoop, calls=%fused_computation.19 | loop fusion | bytes 368640 | tf_op jit(solution)/shard_map/slice | solution.py:22
  1.7 3.8 %collective-permute-start = (bf16[1,180,256]{2,1,0:T(8,128)(2,1)S(1)}, bf16[1,180,256]{2,1,0:T(8,128)(2,1)S(1)}, u32[]{:S(2)}, u32[]{:S(2)}) collective-permute-start(bf16[1,180,256]{2,1,0:T(8,128)(2,1)S(1)} %copy.23), channel_id=1, source_target_pairs={{0,8},{8,16},{16,24},{24,32},{32,40},{40,48},{48,56},{56,64},{64,7... | collective-permute-start | bytes 276488 | tf_op jit(solution)/shard_map/ppermute | solution.py:23
  5.6 4.2 %collective-permute-start.1 = (bf16[1,180,256]{2,1,0:T(8,128)(2,1)S(1)}, bf16[1,180,256]{2,1,0:T(8,128)(2,1)S(1)}, u32[]{:S(2)}, u32[]{:S(2)}) collective-permute-start(bf16[1,180,256]{2,1,0:T(8,128)(2,1)S(1)} %copy.24), channel_id=1, source_target_pairs={{8,0},{16,8},{24,16},{32,24},{40,32},{48,40},{56,48},{64,56},{72,6... | collective-permute-start | bytes 276488 | tf_op jit(solution)/shard_map/ppermute | solution.py:24
  9.8 0.7 compare_and_fusion
  10.5 0.0 collective-permute-done
  10.6 0.0 copy-start.4
  10.6 2.9 %constant_dynamic-update-slice_fusion.1 = bf16[42,180,256]{2,1,0:T(8,128)(2,1)S(1)} fusion(bf16[42,180,256]{2,1,0:T(8,128)(2,1)S(1)} %constant_dynamic-update-slice_fusion.2, bf16[40,180,256]{2,0,1:T(8,128)(2,1)} %param.10), kind=kLoop, calls=%fused_computation.11 | loop fusion | bytes 7454720
  13.5 0.0 collective-permute-done.1
  13.5 0.0 copy-start.2
  13.5 1.9 %copy-done.2 = bf16[42,180,256]{2,1,0:T(8,128)(2,1)} copy-done((bf16[42,180,256]{2,1,0:T(8,128)(2,1)}, bf16[42,180,256]{2,1,0:T(8,128)(2,1)S(1)}, u32[]{:S(2)}) %copy-start.2) | copy-done | bytes 3870744
  15.4 0.1 fusion.5
  15.5 0.0 collective-permute-start.2
  15.5 2.9 %collective-permute-start.3 = (bf16[42,1,256]{2,1,0:T(2,128)(2,1)S(1)}, bf16[42,1,256]{2,1,0:T(2,128)(2,1)S(1)}, u32[]{:S(2)}, u32[]{:S(2)}) collective-permute-start(bf16[42,1,256]{2,1,0:T(2,128)(2,1)S(1)} %get-tuple-element.9), channel_id=1, source_target_pairs={{1,0},{2,1},{3,2},{4,3},{5,4},{6,5},{7,6},{0,7},{9,8},{10,9},{11,1... | collective-permute-start | bytes 64520 | tf_op jit(solution)/shard_map/ppermute | solution.py:24
  18.5 0.0 copy-done
  18.5 0.6 gather_fusion.1
  19.0 1.5 %gather_fusion = f32[2,128]{1,0:T(2,128)S(1)} fusion(f32[720,128]{1,0:T(8,128)} %param.13, s32[1024]{0:T(1024)S(1)} %pad_clamp_fusion), kind=kCustom, calls=%fused_computation.clone | custom fusion | bytes 2056 | tf_op jit(solution)/shard_map/jit(_take)/gather | solution.py:281
  20.6 0.0 copy-start.3
  20.6 0.0 copy-done.4
  20.6 1.0 copy.17
  21.6 0.3 copy.19
  21.9 0.0 copy-start.1
  21.9 0.0 collective-permute-done.2
  21.9 0.0 collective-permute-done.3
  21.9 0.8 copy-done.3
  22.7 2.2 %fusion.4.x_ref = bf16[42,184,256]{2,1,0:T(8,128)(2,1)S(1)} fusion(bf16[42,1,256]{2,1,0:T(2,128)(2,1)S(1)} %collective-permute-done.3, bf16[42,180,256]{2,1,0:T(8,128)(2,1)S(1)} %copy-done.3, bf16[42,1,256]{2,1,0:T(2,128)(2,1)S(1)} %collective-permute-done.2), kind=kLoop, calls=%fused_computation.7 | loop fusion | flops 19783680 | bytes 7870464 | tf_op jit(solution)/shard_map/concatenate | solution.py:25
  24.9 0.0 copy-start.5
  24.9 0.0 copy-done.1
  25.0 16.6 %shard_map.82 = bf16[20,90,128]{2,1,0:T(8,128)(2,1)S(1)} custom-call(bf16[42,184,256]{2,1,0:T(8,128)(2,1)S(1)} %fusion.4.x_ref, bf16[768,768]{1,0:T(8,128)(2,1)S(1)} %bitcast.12, bf16[256,128]{1,0:T(8,128)(2,1)S(1)} %copy-done.1), custom_call_target="tpu_custom_call" | custom-call | tf_op jit(solution)/shard_map/pallas_call | solution.py:89
  41.6 2.4 %collective-permute-start.4 = (bf16[1,90,128]{2,1,0:T(8,128)(2,1)S(1)}, bf16[1,90,128]{2,1,0:T(8,128)(2,1)S(1)}, u32[]{:S(2)}, u32[]{:S(2)}) collective-permute-start(bf16[1,90,128]{2,1,0:T(8,128)(2,1)S(1)} %get-tuple-element.12), channel_id=1, source_target_pairs={{0,8},{8,16},{16,24},{24,32},{32,40},{40,48},{48,56},{56,64},{64,7... | collective-permute-start | bytes 69128 | tf_op jit(solution)/shard_map/ppermute | solution.py:23
  44.0 5.6 %collective-permute-start.5 = (bf16[1,90,128]{2,1,0:T(8,128)(2,1)S(1)}, bf16[1,90,128]{2,1,0:T(8,128)(2,1)S(1)}, u32[]{:S(2)}, u32[]{:S(2)}) collective-permute-start(bf16[1,90,128]{2,1,0:T(8,128)(2,1)S(1)} %get-tuple-element.13), channel_id=1, source_target_pairs={{8,0},{16,8},{24,16},{32,24},{40,32},{48,40},{56,48},{64,56},{72,6... | collective-permute-start | bytes 69128 | tf_op jit(solution)/shard_map/ppermute | solution.py:24
  49.6 0.7 broadcast_select_fusion
  50.2 0.0 copy-done.5
  50.2 0.3 copy.18
  50.5 0.8 copy.25
  51.3 0.0 collective-permute-done.4
  51.3 0.0 collective-permute-done.5
  51.3 0.9 pad_maximum_fusion.tile_ref
  52.1 47.0 %shard_map.83 = bf16[2,20,720,128]{3,2,1,0:T(8,128)(2,1)} custom-call(bf16[22,90,128]{2,1,0:T(8,128)(2,1)} %pad_maximum_fusion.tile_ref, f32[2,1,128]{2,1,0:T(1,128)} %bitcast.19, f32[2,1,128]{2,1,0:T(1,128)} %bitcast.18, bf16[384,384]{1,0:T(8,128)(2,1)} %bitcast.15, bf16[720,720]{1,0:T(8,128)(2,1)} %mix_ref.1), custom_call_target="tpu_custom_call" | custom-call | tf_op jit(solution)/shard_map/pallas_call | solution.py:252
  99.2 6.6 %copy.29 = bf16[2,20,720,128]{3,2,1,0:T(8,128)(2,1)} copy(bf16[2,20,720,128]{3,2,1,0:T(8,128)(2,1)} %shard_map.83) | data formatting | bytes 14745600
  (6 shorter events, 0.1 us)
Async XLA Ops:
  0.0 18.5 %copy-start = (f32[720,128]{1,0:T(8,128)S(1)}, f32[720,128]{1,0:T(8,128)}, u32[]{:S(2)}) copy-start(f32[720,128]{1,0:T(8,128)} %param.14) | copy-start | bytes 1105924
  1.7 8.8 %collective-permute-start = (bf16[1,180,256]{2,1,0:T(8,128)(2,1)S(1)}, bf16[1,180,256]{2,1,0:T(8,128)(2,1)S(1)}, u32[]{:S(2)}, u32[]{:S(2)}) collective-permute-start(bf16[1,180,256]{2,1,0:T(8,128)(2,1)S(1)} %copy.23), channel_id=1, source_target_pairs={{0,8},{8,16},{16,24},{24,32},{32,40},{40,48},{48,56},{56,64},{64,7... | collective-permute-start | bytes 276488 | tf_op jit(solution)/shard_map/ppermute | solution.py:23
  5.6 7.9 %collective-permute-start.1 = (bf16[1,180,256]{2,1,0:T(8,128)(2,1)S(1)}, bf16[1,180,256]{2,1,0:T(8,128)(2,1)S(1)}, u32[]{:S(2)}, u32[]{:S(2)}) collective-permute-start(bf16[1,180,256]{2,1,0:T(8,128)(2,1)S(1)} %copy.24), channel_id=1, source_target_pairs={{8,0},{16,8},{24,16},{32,24},{40,32},{48,40},{56,48},{64,56},{72,6... | collective-permute-start | bytes 276488 | tf_op jit(solution)/shard_map/ppermute | solution.py:24
  10.6 10.0 %copy-start.4 = (bf16[3,3,256,256]{3,2,1,0:T(8,128)(2,1)S(1)}, bf16[3,3,256,256]{3,2,1,0:T(8,128)(2,1)}, u32[]{:S(2)}) copy-start(bf16[3,3,256,256]{3,2,1,0:T(8,128)(2,1)} %param.11) | copy-start | bytes 3538948
  13.5 1.9 %copy-start.2 = (bf16[42,180,256]{2,1,0:T(8,128)(2,1)}, bf16[42,180,256]{2,1,0:T(8,128)(2,1)S(1)}, u32[]{:S(2)}) copy-start(bf16[42,180,256]{2,1,0:T(8,128)(2,1)S(1)} %constant_dynamic-update-slice_fusion) | copy-start | bytes 11612164
  15.5 6.4 %collective-permute-start.2 = (bf16[42,1,256]{2,1,0:T(2,128)(2,1)S(1)}, bf16[42,1,256]{2,1,0:T(2,128)(2,1)S(1)}, u32[]{:S(2)}, u32[]{:S(2)}) collective-permute-start(bf16[42,1,256]{2,1,0:T(2,128)(2,1)S(1)} %get-tuple-element.8), channel_id=1, source_target_pairs={{0,1},{1,2},{2,3},{3,4},{4,5},{5,6},{6,7},{7,0},{8,9},{9,10},{10,1... | collective-permute-start | bytes 64520 | tf_op jit(solution)/shard_map/ppermute | solution.py:23
  15.5 6.4 %collective-permute-start.3 = (bf16[42,1,256]{2,1,0:T(2,128)(2,1)S(1)}, bf16[42,1,256]{2,1,0:T(2,128)(2,1)S(1)}, u32[]{:S(2)}, u32[]{:S(2)}) collective-permute-start(bf16[42,1,256]{2,1,0:T(2,128)(2,1)S(1)} %get-tuple-element.9), channel_id=1, source_target_pairs={{1,0},{2,1},{3,2},{4,3},{5,4},{6,5},{7,6},{0,7},{9,8},{10,9},{11,1... | collective-permute-start | bytes 64520 | tf_op jit(solution)/shard_map/ppermute | solution.py:24
  20.6 2.1 %copy-start.3 = (bf16[42,180,256]{2,1,0:T(8,128)(2,1)S(1)}, bf16[42,180,256]{2,1,0:T(8,128)(2,1)}, u32[]{:S(2)}) copy-start(bf16[42,180,256]{2,1,0:T(8,128)(2,1)} %copy-done.2) | copy-start | bytes 11612164
  21.9 3.0 %copy-start.1 = (bf16[256,128]{1,0:T(8,128)(2,1)S(1)}, bf16[256,128]{1,0:T(8,128)(2,1)}, u32[]{:S(2)}) copy-start(bf16[256,128]{1,0:T(8,128)(2,1)} %proj_ref.1) | copy-start | bytes 196612
  24.9 25.3 %copy-start.5 = (bf16[3,3,128,128]{3,2,1,0:T(8,128)(2,1)S(1)}, bf16[3,3,128,128]{3,2,1,0:T(8,128)(2,1)}, u32[]{:S(2)}) copy-start(bf16[3,3,128,128]{3,2,1,0:T(8,128)(2,1)} %param.16) | copy-start | bytes 884740
  41.6 9.7 %collective-permute-start.4 = (bf16[1,90,128]{2,1,0:T(8,128)(2,1)S(1)}, bf16[1,90,128]{2,1,0:T(8,128)(2,1)S(1)}, u32[]{:S(2)}, u32[]{:S(2)}) collective-permute-start(bf16[1,90,128]{2,1,0:T(8,128)(2,1)S(1)} %get-tuple-element.12), channel_id=1, source_target_pairs={{0,8},{8,16},{16,24},{24,32},{32,40},{40,48},{48,56},{56,64},{64,7... | collective-permute-start | bytes 69128 | tf_op jit(solution)/shard_map/ppermute | solution.py:23
  44.0 7.3 %collective-permute-start.5 = (bf16[1,90,128]{2,1,0:T(8,128)(2,1)S(1)}, bf16[1,90,128]{2,1,0:T(8,128)(2,1)S(1)}, u32[]{:S(2)}, u32[]{:S(2)}) collective-permute-start(bf16[1,90,128]{2,1,0:T(8,128)(2,1)S(1)} %get-tuple-element.13), channel_id=1, source_target_pairs={{8,0},{16,8},{24,16},{32,24},{40,32},{48,40},{56,48},{64,56},{72,6... | collective-permute-start | bytes 69128 | tf_op jit(solution)/shard_map/ppermute | solution.py:24

commit v7 on v6

--- a/solution.py
+++ b/solution.py
@@ -46,22 +46,107 @@
     return summed * 0.25
 
 
-def encoder_kernel(x_ref, w_ref, proj_ref, out_ref, pair_ref):
-    cols = x_ref.shape[1]
-    width = x_ref.shape[2]
-    pooled_cols = out_ref.shape[1]
+def encoder_kernel(x_hbm, w_ref, proj_ref, out_ref, xpad, pair_ref, local_sem, send_sem, recv_sem):
+    lat = lax.axis_index("lat")
+    lon = lax.axis_index("lon")
+    lats = lax.axis_size("lat")
+    lons = lax.axis_size("lon")
+    has_up = lat > 0
+    has_down = lat < lats - 1
+    up, down = lat - 1, lat + 1
+    left, right = lax.rem(lon + lons - 1, lons), lax.rem(lon + 1, lons)
+    rows, tile_cols, width = x_hbm.shape
+    cols = xpad.shape[2]
+    pooled_rows, pooled_cols = rows // 2, tile_cols // 2
+
+    barrier = pltpu.get_barrier_semaphore()
+
+    @pl.when(has_up)
+    def _():
+        pl.semaphore_signal(barrier, inc=1, device_id=(up, lon), device_id_type=MESH)
+
+    @pl.when(has_down)
+    def _():
+        pl.semaphore_signal(barrier, inc=1, device_id=(down, lon), device_id_type=MESH)
+
+    for peer in (left, right):
+        pl.semaphore_signal(barrier, inc=1, device_id=(lat, peer), device_id_type=MESH)
+    pl.semaphore_wait(barrier, 2 + has_up.astype(jnp.int32) + has_down.astype(jnp.int32))
+
+    def remote(kind, src, dst, target):
+        return pltpu.make_async_remote_copy(
+            src_ref=src, dst_ref=dst, send_sem=send_sem.at[kind], recv_sem=recv_sem.at[kind],
+            device_id=target, device_id_type=MESH,
+        )
+
+    halves = xpad.shape[1]
+    lanes = xpad.shape[3]
+    inner = pl.ds(0, tile_cols)
+    locals_ = []
+    to_up, to_down = [], []
+    for h in range(halves):
+        part = pl.ds(h * lanes, lanes)
+        locals_.append(
+            pltpu.make_async_copy(x_hbm.at[:, :, part], xpad.at[pl.ds(1, rows), h, inner], local_sem.at[h])
+        )
+        to_up.append(remote(h, x_hbm.at[0, :, part], xpad.at[rows + 1, h, inner], (up, lon)))
+        to_down.append(remote(2 + h, x_hbm.at[rows - 1, :, part], xpad.at[0, h, inner], (down, lon)))
+    for h in range(halves):
+        locals_[h].start()
+        pl.when(has_up)(to_up[h].start)
+        pl.when(has_down)(to_down[h].start)
+
+    def zero_edges(first, count):
+        span = pl.ds(first, count)
+
+        @pl.when(lat == 0)
+        def _():
+            xpad[0, :, span] = jnp.zeros((halves, count, lanes), xpad.dtype)
+
+        @pl.when(lat == lats - 1)
+        def _():
+            xpad[rows + 1, :, span] = jnp.zeros((halves, count, lanes), xpad.dtype)
+
+    for h in range(halves):
+        locals_[h].wait()
+        pl.when(has_down)(to_up[h].wait_recv)
+        pl.when(has_up)(to_down[h].wait_recv)
+    zero_edges(0, tile_cols)
+    to_left, to_right = [], []
+    for h in range(halves):
+        pair_cols = pl.ds(0, 2)
+        to_left.append(
+            remote(4 + h, xpad.at[:, h, pair_cols], xpad.at[:, h, pl.ds(tile_cols, 2)], (lat, left))
+        )
+        to_right.append(
+            remote(
+                6 + h,
+                xpad.at[:, h, pl.ds(tile_cols - 2, 2)],
+                xpad.at[:, h, pl.ds(cols - 2, 2)],
+                (lat, right),
+            )
+        )
+    for h in range(halves):
+        to_left[h].start()
+        to_right[h].start()
+    for h in range(halves):
+        to_left[h].wait_recv()
+        to_right[h].wait_recv()
+    zero_edges(tile_cols, cols - tile_cols)
 
     def encoded(row):
-        stacked = jnp.concatenate([x_ref[row + k] for k in range(3)], axis=-1)
+        stacked = jnp.concatenate(
+            [xpad[row + k, h] for k in range(3) for h in range(halves)], axis=-1
+        )
         taps = jnp.dot(stacked, w_ref[...], preferred_element_type=jnp.float32)
         conv = (
-            taps[:, :width]
-            + pltpu.roll(taps[:, width : 2 * width], cols - 1, 0)
-            + pltpu.roll(taps[:, 2 * width :], cols - 2, 0)
+            pltpu.roll(taps[:, :width], 1, 0)
+            + taps[:, width : 2 * width]
+            + pltpu.roll(taps[:, 2 * width :], cols - 1, 0)
         )
         return jax.nn.gelu(conv)
 
-    def one_row(p, carry):
+    def pooled_row(p):
         pair = encoded(2 * p) + encoded(2 * p + 1)
         lanes = pair_ref.shape[2]
         chunks = []
@@ -75,25 +160,61 @@
         summed = jnp.concatenate(chunks, axis=-1)
         pooled = (summed * 0.25).astype(jnp.bfloat16)
         projected = jnp.dot(pooled, proj_ref[...], preferred_element_type=jnp.float32)
-        out_ref[p] = projected[:pooled_cols].astype(out_ref.dtype)
+        out_ref[p + 1] = projected[:pooled_cols].astype(out_ref.dtype)
+
+    pooled_row(0)
+    edge_up = remote(8, out_ref.at[1], out_ref.at[pooled_rows + 1], (up, lon))
+    pl.when(has_up)(edge_up.start)
+    pooled_row(pooled_rows - 1)
+    edge_down = remote(9, out_ref.at[pooled_rows], out_ref.at[0], (down, lon))
+    pl.when(has_down)(edge_down.start)
+
+    def one_row(p, carry):
+        pooled_row(p)
         return carry
 
-    lax.fori_loop(0, out_ref.shape[0], one_row, 0)
-
-
-def encoder(padded, w_enc, w_proj):
-    rows, cols, width = padded.shape
-    pooled_rows, pooled_cols = (rows - 2) // 2, (cols - 4) // 2
+    lax.fori_loop(1, pooled_rows - 1, one_row, 0)
+    pl.when(has_down)(edge_up.wait_recv)
+    pl.when(has_up)(edge_down.wait_recv)
+
+    @pl.when(lat == 0)
+    def _():
+        out_ref[0] = jnp.zeros(out_ref.shape[1:], out_ref.dtype)
+
+    @pl.when(lat == lats - 1)
+    def _():
+        out_ref[pooled_rows + 1] = jnp.zeros(out_ref.shape[1:], out_ref.dtype)
+
+    for h in range(halves):
+        pl.when(has_up)(to_up[h].wait_send)
+        pl.when(has_down)(to_down[h].wait_send)
+        to_left[h].wait_send()
+        to_right[h].wait_send()
+    pl.when(has_up)(edge_up.wait_send)
+    pl.when(has_down)(edge_down.wait_send)
+
+
+def encoder(tile, w_enc, w_proj):
+    rows, tile_cols, width = tile.shape
+    cols = tile_cols + 4
     w_all = jnp.transpose(w_enc, (0, 2, 1, 3)).reshape(3 * width, 3 * width)
     vmem = pl.BlockSpec(memory_space=pltpu.VMEM)
     return pl.pallas_call(
         encoder_kernel,
-        out_shape=jax.ShapeDtypeStruct((pooled_rows, pooled_cols, w_proj.shape[1]), jnp.bfloat16),
-        in_specs=[vmem, vmem, vmem],
+        out_shape=jax.ShapeDtypeStruct((rows // 2 + 2, tile_cols // 2, w_proj.shape[1]), jnp.bfloat16),
+        in_specs=[pl.BlockSpec(memory_space=pl.ANY), vmem, vmem],
         out_specs=vmem,
-        scratch_shapes=[pltpu.VMEM((width // 128, cols + 8, 128), jnp.float32)],
-        compiler_params=pltpu.CompilerParams(vmem_limit_bytes=48 * 1024 * 1024),
-    )(padded, w_all, w_proj)
+        scratch_shapes=[
+            pltpu.VMEM((rows + 2, width // 128, cols, 128), jnp.bfloat16),
+            pltpu.VMEM((width // 128, cols + 8, 128), jnp.float32),
+            pltpu.SemaphoreType.DMA((width // 128,)),
+            pltpu.SemaphoreType.DMA((10,)),
+            pltpu.SemaphoreType.DMA((10,)),
+        ],
+        compiler_params=pltpu.CompilerParams(
+            collective_id=1, has_side_effects=True, vmem_limit_bytes=48 * 1024 * 1024
+        ),
+    )(tile, w_all, w_proj)
 
 
 def head_kernel(tile_ref, scale_ref, shift_ref, w_ref, mix_ref, out_ref, band_ref, mod_ref,
@@ -270,14 +391,10 @@
 
 def shards(inputs, w_enc, w_proj, film_scale, film_shift, lead_ids, w_head, zonal_mix):
     lat_rows, lon_cols, channels = inputs.shape
-    with_rows = extended(inputs, (("lat", 0),), 1, False)
-    padded = extended(with_rows, (("lon", 1),), 1, True)
-    padded = jnp.pad(padded, ((0, 0), (0, 2), (0, 0)))
-    tile = encoder(padded, w_enc, w_proj)
+    tile = encoder(inputs, w_enc, w_proj)
     head_width = w_proj.shape[1]
     lon_group = lax.axis_index("lon")
     my_rows = lax.dynamic_slice_in_dim(lead_ids, lon_group * LEAD_DEV, LEAD_DEV)
-    tile = extended(tile, (("lat", 0),), 1, False)
     scales = jnp.take(film_scale, my_rows, axis=0)
     shifts = jnp.take(film_shift, my_rows, axis=0)
     w_all = jnp.transpose(w_head, (0, 2, 1, 3)).reshape(3 * head_width, 3 * head_width)

time: 106 us -> 94.1 us (0.89)
  starting transfers between devices: 19 us -> 0 us
  Pallas kernels: 63.7 us -> 76.9 us
  other arithmetic: 4.51 us -> 1.44 us
  local copies, waits for them, and re-layouts: 18.4 us -> 15.4 us
    ppermute x6 -> x0, starting transfers between devices: 19 us -> none  [the longest x3 12.7 us: extended(): after = lax.ppermute(initial, axis, down)]
    pallas_call x1, Pallas kernels: 16.6 us -> 28.5 us  [encoder(): pl.pallas_call(encoder_kernel, out_shape=jax.ShapeDtypeStruct((rows // 2...]
    unnamed x19 -> x12, local copies, waits for them, and re-layouts: 13.3 us -> 9.49 us
    concatenate x2 -> x0, other arithmetic: 3.1 us -> none  [extended(): x = jnp.concatenate([before, x, after], axis=dim)]
    slice x3 -> x0, local copies, waits for them, and re-layouts: 1.76 us -> none  [the longest x1 1.69 us: extended(): initial = lax.slice_in_dim(x, 0, width, axis=dim)]
    pallas_call x1, Pallas kernels: 47 us -> 48.4 us  [head(): pl.pallas_call(head_kernel, out_shape=jax.ShapeDtypeStruct((leads, rows,...]
    transpose x1, local copies, waits for them, and re-layouts: 0.26 us -> 1.55 us  [shards(): jnp.transpose(w_head, (0, 2, 1, 3)).reshape(3 * head_width, 3 * head_width)]
    transpose x1, local copies, waits for them, and re-layouts: 1.01 us -> 2.28 us  [encoder(): w_all = jnp.transpose(w_enc, (0, 2, 1, 3)).reshape(3 * width, 3 * width)]
  transfers between devices with their start and end apart: 6 -> 0, of which waited for: 0 -> 0; matrix products, arithmetic and copies ran while one was open for 8% -> 0% of each run, Pallas kernels for 0% -> 0%
where the time goes in v7:
time: 94.1 us; the launch traced here: 93.8 us
  Pallas kernels  76.9 us (82%)
  local copies, waits for them, and re-layouts  15.4 us (16%)
  other arithmetic  1.44 us (2%)
    pallas_call x1, Pallas kernels, head(): pl.pallas_call(head_kernel, out_shape=jax.ShapeDtypeStruct((leads, rows,...  48.4 us
    pallas_call x1, Pallas kernels, encoder(): pl.pallas_call(encoder_kernel, out_shape=jax.ShapeDtypeStruct((rows // 2...  28.5 us
    unnamed x12, local copies, waits for them, and re-layouts  9.49 us
    transpose x1, local copies, waits for them, and re-layouts, encoder(): w_all = jnp.transpose(w_enc, (0, 2, 1, 3)).reshape(3 * width, 3 * width)  2.28 us

profile of v7, /device:TPU:24, one launch (start us, length us, event | category | flops | bytes accessed | tf_op | source)
XLA Modules:
  0.0 93.8 jit_solution(7485063592149585774)
XLA Ops:
  0.0 0.0 copy-start
  0.0 0.8 compare_and_fusion
  0.8 0.2 copy-done
  1.0 0.6 gather_fusion.1
  1.6 1.5 %gather_fusion = f32[2,128]{1,0:T(2,128)S(1)} fusion(f32[720,128]{1,0:T(8,128)} %param.13, s32[1024]{0:T(1024)S(1)} %pad_clamp_fusion), kind=kCustom, calls=%fused_computation.clone | custom fusion | bytes 2056 | tf_op jit(solution)/shard_map/jit(_take)/gather | solution.py:398
  3.1 0.0 copy-start.3
  3.1 0.7 broadcast_select_fusion
  3.8 1.5 %copy.14 = bf16[3,128,3,128]{3,2,1,0:T(4,128)(2,1)S(1)} copy(bf16[3,128,3,128]{3,1,2,0:T(8,128)(2,1)} %bitcast.17) | data formatting | bytes 589824 | tf_op jit(solution)/shard_map/transpose | solution.py:400
  5.3 0.7 copy.18
  6.1 2.3 %copy.12 = bf16[3,256,3,256]{3,2,1,0:T(4,128)(2,1)S(1)} copy(bf16[3,256,3,256]{3,1,2,0:T(8,128)(2,1)} %bitcast.16) | data formatting | bytes 2359296 | tf_op jit(solution)/shard_map/transpose | solution.py:200
  8.4 0.3 copy.15
  8.6 0.0 copy-done.3
  8.6 0.0 copy-start.2
  8.7 0.7 copy.13.x_hbm
  9.4 0.1 copy-done.2
  9.5 28.5 %shard_map.82.tile_ref = bf16[22,90,128]{2,1,0:T(8,128)(2,1)S(1)} custom-call(bf16[40,180,256]{2,1,0:T(8,128)(2,1)S(1)} %copy.13.x_hbm, bf16[768,768]{1,0:T(8,128)(2,1)S(1)} %bitcast.12, bf16[256,128]{1,0:T(8,128)(2,1)S(1)} %copy-done.2), custom_call_target="tpu_custom_call" | custom-call | tf_op jit(solution)/shard_map/pallas_call | solution.py:202
  38.0 0.0 copy-start.1
  38.0 0.8 copy-done.1
  38.8 48.4 %shard_map.83 = bf16[2,20,720,128]{3,2,1,0:T(8,128)(2,1)} custom-call(bf16[22,90,128]{2,1,0:T(8,128)(2,1)} %copy-done.1, f32[2,1,128]{2,1,0:T(1,128)} %bitcast.19, f32[2,1,128]{2,1,0:T(1,128)} %bitcast.18, bf16[384,384]{1,0:T(8,128)(2,1)} %bitcast.15, bf16[720,720]{1,0:T(8,128)(2,1)} %mix_ref.1), custom_call_target="tpu_custom_call" | custom-call | tf_op jit(solution)/shard_map/pallas_call | solution.py:373
  87.2 6.6 %copy.20 = bf16[2,20,720,128]{3,2,1,0:T(8,128)(2,1)} copy(bf16[2,20,720,128]{3,2,1,0:T(8,128)(2,1)} %shard_map.83) | data formatting | bytes 14745600
  (1 shorter events, 0.0 us)
Async XLA Ops:
  0.0 1.0 %copy-start = (f32[720,128]{1,0:T(8,128)S(1)}, f32[720,128]{1,0:T(8,128)}, u32[]{:S(2)}) copy-start(f32[720,128]{1,0:T(8,128)} %param.14) | copy-start | bytes 1105924
  3.1 5.5 %copy-start.3 = (bf16[40,180,256]{2,0,1:T(8,128)(2,1)S(1)}, bf16[40,180,256]{2,0,1:T(8,128)(2,1)}, u32[]{:S(2)}) copy-start(bf16[40,180,256]{2,0,1:T(8,128)(2,1)} %param.10) | copy-start | bytes 11059204
  8.6 0.8 copy-start.2
  38.0 0.8 copy-start.1

commit v8 on v7

--- a/solution.py
+++ b/solution.py
@@ -46,7 +46,7 @@
     return summed * 0.25
 
 
-def encoder_kernel(x_hbm, w_ref, proj_ref, out_ref, xpad, pair_ref, local_sem, send_sem, recv_sem):
+def encoder_kernel(x_hbm, w_in, proj_ref, out_ref, xpad, pair_ref, w_ref, local_sem, send_sem, recv_sem):
     lat = lax.axis_index("lat")
     lon = lax.axis_index("lon")
     lats = lax.axis_size("lat")
@@ -107,6 +107,10 @@
         def _():
             xpad[rows + 1, :, span] = jnp.zeros((halves, count, lanes), xpad.dtype)
 
+    taps_n = w_in.shape[0]
+    for di in range(taps_n):
+        for dj in range(taps_n):
+            w_ref[di * width : (di + 1) * width, dj * width : (dj + 1) * width] = w_in[di, dj]
     for h in range(halves):
         locals_[h].wait()
         pl.when(has_down)(to_up[h].wait_recv)
@@ -197,7 +201,6 @@
 def encoder(tile, w_enc, w_proj):
     rows, tile_cols, width = tile.shape
     cols = tile_cols + 4
-    w_all = jnp.transpose(w_enc, (0, 2, 1, 3)).reshape(3 * width, 3 * width)
     vmem = pl.BlockSpec(memory_space=pltpu.VMEM)
     return pl.pallas_call(
         encoder_kernel,
@@ -207,6 +210,7 @@
         scratch_shapes=[
             pltpu.VMEM((rows + 2, width // 128, cols, 128), jnp.bfloat16),
             pltpu.VMEM((width // 128, cols + 8, 128), jnp.float32),
+            pltpu.VMEM((3 * width, 3 * width), jnp.bfloat16),
             pltpu.SemaphoreType.DMA((width // 128,)),
             pltpu.SemaphoreType.DMA((10,)),
             pltpu.SemaphoreType.DMA((10,)),
@@ -214,11 +218,11 @@
         compiler_params=pltpu.CompilerParams(
             collective_id=1, has_side_effects=True, vmem_limit_bytes=48 * 1024 * 1024
         ),
-    )(tile, w_all, w_proj)
-
-
-def head_kernel(tile_ref, scale_ref, shift_ref, w_ref, mix_ref, out_ref, band_ref, mod_ref,
-                hidden_ref, send_sem, recv_sem, local_sem):
+    )(tile, w_enc, w_proj)
+
+
+def head_kernel(ids_ref, tile_ref, scale_ref, shift_ref, w_in, mix_ref, out_ref, band_ref, mod_ref,
+                hidden_ref, w_ref, send_sem, recv_sem, local_sem):
     me = lax.axis_index("lon")
     n = lax.axis_size("lon")
     lat = lax.axis_index("lat")
@@ -308,6 +312,15 @@
 
     for piece in range(min(AHEAD + 3, pieces)):
         direct(piece)
+    taps_n = w_in.shape[0]
+    for di in range(taps_n):
+        for dj in range(taps_n):
+            w_ref[di * width : (di + 1) * width, dj * width : (dj + 1) * width] = w_in[di, dj]
+    gains, shifts = [], []
+    for l in range(leads):
+        row = ids_ref[leads * me + l]
+        gains.append(1.0 + scale_ref[pl.ds(row, 1), :])
+        shifts.append(shift_ref[pl.ds(row, 1), :])
     for piece in range(min(3, pieces)):
         forward_x(piece)
     for piece in range(min(2, pieces)):
@@ -330,8 +343,8 @@
         arrived(k + 1)
         base = k * step
         for l in range(leads):
-            gain = 1.0 + scale_ref[l]
-            shift = shift_ref[l]
+            gain = gains[l]
+            shift = shifts[l]
             for j in range(step + 2):
                 row = base + j
                 keep = ((row > 0) | (lat > 0)) & ((row < halo_rows - 1) | (lat < last_lat))
@@ -363,22 +376,23 @@
             copy.wait_send()
 
 
-def head(tile, scales, shifts, w_all, zonal_mix, lon_devices):
+def head(lead_ids, tile, film_scale, film_shift, w_head, zonal_mix, lon_devices):
     halo_rows, tile_cols, width = tile.shape
     rows = halo_rows - 2
     cols = tile_cols * lon_devices
-    leads = scales.shape[0]
+    leads = LEAD_DEV
     pieces = halo_rows // HEAD_ROWS
     vmem = pl.BlockSpec(memory_space=pltpu.VMEM)
     return pl.pallas_call(
         head_kernel,
         out_shape=jax.ShapeDtypeStruct((leads, rows, cols, width), jnp.bfloat16),
-        in_specs=[pl.BlockSpec(memory_space=pl.ANY), vmem, vmem, vmem, vmem],
+        in_specs=[pl.BlockSpec(memory_space=pltpu.SMEM), pl.BlockSpec(memory_space=pl.ANY), vmem, vmem, vmem, vmem],
         out_specs=vmem,
         scratch_shapes=[
             pltpu.VMEM((halo_rows, cols, width), jnp.bfloat16),
             pltpu.VMEM((leads, HEAD_ROWS + 2, cols, width), jnp.bfloat16),
             pltpu.VMEM((cols, leads * HEAD_ROWS * width), jnp.bfloat16),
+            pltpu.VMEM((3 * width, 3 * width), jnp.bfloat16),
             pltpu.SemaphoreType.DMA((pieces * 7,)),
             pltpu.SemaphoreType.DMA((pieces * 7,)),
             pltpu.SemaphoreType.DMA((pieces,)),
@@ -386,19 +400,13 @@
         compiler_params=pltpu.CompilerParams(
             collective_id=0, has_side_effects=True, vmem_limit_bytes=56 * 1024 * 1024
         ),
-    )(tile, scales[:, None, :], shifts[:, None, :], w_all, zonal_mix)
+    )(lead_ids, tile, film_scale, film_shift, w_head, zonal_mix)
 
 
 def shards(inputs, w_enc, w_proj, film_scale, film_shift, lead_ids, w_head, zonal_mix):
     lat_rows, lon_cols, channels = inputs.shape
     tile = encoder(inputs, w_enc, w_proj)
-    head_width = w_proj.shape[1]
-    lon_group = lax.axis_index("lon")
-    my_rows = lax.dynamic_slice_in_dim(lead_ids, lon_group * LEAD_DEV, LEAD_DEV)
-    scales = jnp.take(film_scale, my_rows, axis=0)
-    shifts = jnp.take(film_shift, my_rows, axis=0)
-    w_all = jnp.transpose(w_head, (0, 2, 1, 3)).reshape(3 * head_width, 3 * head_width)
-    return head(tile, scales, shifts, w_all, zonal_mix, lax.axis_size("lon"))
+    return head(lead_ids, tile, film_scale, film_shift, w_head, zonal_mix, lax.axis_size("lon"))
 
 def solution(mesh):
     in_specs = (P("lat", "lon", None), P(), P(), P(), P(), P(), P(), P())

time: 94.1 us -> 87.9 us (0.934)
  local copies, waits for them, and re-layouts: 15.4 us -> 10.3 us
  other arithmetic: 1.44 us -> 0 us
    transpose x2 -> x0, local copies, waits for them, and re-layouts: 3.83 us -> none  [the longest x1 2.28 us: encoder(): w_all = jnp.transpose(w_enc, (0, 2, 1, 3)).reshape(3 * width, 3 * width)]
    gather x2 -> x0, local copies, waits for them, and re-layouts: 2.1 us -> none  [the longest x1 1.54 us: shards(): scales = jnp.take(film_scale, my_rows, axis=0)]
    unnamed x12 -> x8, local copies, waits for them, and re-layouts: 9.49 us -> 10.3 us
where the time goes in v8:
time: 87.9 us; the launch traced here: 87.7 us
  Pallas kernels  77.4 us (88%)
  local copies, waits for them, and re-layouts  10.3 us (12%)
    pallas_call x1, Pallas kernels, head(): pl.pallas_call(head_kernel, out_shape=jax.ShapeDtypeStruct((leads, rows,...  48.9 us
    pallas_call x1, Pallas kernels, encoder(): pl.pallas_call(encoder_kernel, out_shape=jax.ShapeDtypeStruct((rows // 2...  28.5 us
    unnamed x8, local copies, waits for them, and re-layouts  10.3 us

profile of v8, /device:TPU:24, one launch (start us, length us, event | category | flops | bytes accessed | tf_op | source)
XLA Modules:
  0.0 87.7 jit_solution(8200187400020695458)
XLA Ops:
  0.0 0.0 copy-start.2
  0.0 0.0 copy-start.1
  0.0 2.9 %copy.9.x_hbm = bf16[40,180,256]{2,1,0:T(8,128)(2,1)S(1)} copy(bf16[40,180,256]{2,0,1:T(8,128)(2,1)} %param.8) | data formatting | bytes 7372800 | tf_op args[0]
  2.9 0.0 copy-done.2
  2.9 0.0 copy-done.1
  2.9 28.5 %shard_map.82.tile_ref = bf16[22,90,128]{2,1,0:T(8,128)(2,1)S(1)} custom-call(bf16[40,180,256]{2,1,0:T(8,128)(2,1)S(1)} %copy.9.x_hbm, bf16[3,3,256,256]{3,2,1,0:T(8,128)(2,1)S(1)} %copy-done.1, bf16[256,128]{1,0:T(8,128)(2,1)S(1)} %copy-done.2), custom_call_target="tpu_custom_call" | custom-call | tf_op jit(solution)/shard_map/pallas_call | solution.py:205
  31.5 0.0 copy-start
  31.5 0.8 copy-done
  32.3 48.9 %shard_map.83 = bf16[2,20,720,128]{3,2,1,0:T(8,128)(2,1)} custom-call(s32[16]{0:T(128)} %ids_ref.1, bf16[22,90,128]{2,1,0:T(8,128)(2,1)} %copy-done, f32[720,128]{1,0:T(8,128)} %scale_ref.1, f32[720,128]{1,0:T(8,128)} %shift_ref.1, bf16[3,3,128,128]{3,2,1,0:T(8,128)(2,1)} %w_in.3, bf16[720,720]{1,0:T(8,128)(2,1)} %mix_ref.1), custom_call_target="tpu_custom_call" | custom-call | tf_op jit(solution)/shard_map/pallas_call | solution.py:386
  81.1 6.6 %copy.11 = bf16[2,20,720,128]{3,2,1,0:T(8,128)(2,1)} copy(bf16[2,20,720,128]{3,2,1,0:T(8,128)(2,1)} %shard_map.83) | data formatting | bytes 14745600
Async XLA Ops:
  0.0 2.9 %copy-start.2 = (bf16[256,128]{1,0:T(8,128)(2,1)S(1)}, bf16[256,128]{1,0:T(8,128)(2,1)}, u32[]{:S(2)}) copy-start(bf16[256,128]{1,0:T(8,128)(2,1)} %proj_ref.1) | copy-start | bytes 196612
  0.0 2.9 %copy-start.1 = (bf16[3,3,256,256]{3,2,1,0:T(8,128)(2,1)S(1)}, bf16[3,3,256,256]{3,2,1,0:T(8,128)(2,1)}, u32[]{:S(2)}) copy-start(bf16[3,3,256,256]{3,2,1,0:T(8,128)(2,1)} %w_in.2) | copy-start | bytes 3538948
  31.5 0.8 copy-start

commit v9 on v8

--- a/solution.py
+++ b/solution.py
@@ -10,6 +10,7 @@
 LEAD_DEV = 2
 HEAD_ROWS = 2
 AHEAD = 1
+VMEM_ALL = 67043328
 MESH = pl.DeviceIdType.MESH
 
 
@@ -216,7 +217,7 @@
             pltpu.SemaphoreType.DMA((10,)),
         ],
         compiler_params=pltpu.CompilerParams(
-            collective_id=1, has_side_effects=True, vmem_limit_bytes=48 * 1024 * 1024
+            collective_id=1, has_side_effects=True, vmem_limit_bytes=VMEM_ALL
         ),
     )(tile, w_enc, w_proj)
 
@@ -327,6 +328,17 @@
         forward_sibling(piece)
     arrived(0)
 
+    def modulate(piece):
+        for j in range(step):
+            row = piece * step + j
+            keep = ((row > 0) | (lat > 0)) & ((row < halo_rows - 1) | (lat < last_lat))
+            source = band_ref[row].astype(jnp.float32)
+            for l in range(leads):
+                value = jnp.where(keep, source * gains[l] + shifts[l], 0.0)
+                mod_ref[l, row] = value.astype(jnp.bfloat16)
+
+    modulate(0)
+
     def one_chunk(k, carry):
         @pl.when(k + AHEAD + 3 < pieces)
         def _():
@@ -341,18 +353,11 @@
             forward_sibling(k + 2)
 
         arrived(k + 1)
+        modulate(k + 1)
         base = k * step
         for l in range(leads):
-            gain = gains[l]
-            shift = shifts[l]
-            for j in range(step + 2):
-                row = base + j
-                keep = ((row > 0) | (lat > 0)) & ((row < halo_rows - 1) | (lat < last_lat))
-                value = band_ref[row].astype(jnp.float32) * gain + shift
-                value = jnp.where(keep, value, 0.0)
-                mod_ref[l, j] = value.astype(jnp.bfloat16)
             for j in range(step):
-                stacked = jnp.concatenate([mod_ref[l, j + t] for t in range(3)], axis=-1)
+                stacked = jnp.concatenate([mod_ref[l, base + j + t] for t in range(3)], axis=-1)
                 taps = jnp.dot(stacked, w_ref[...], preferred_element_type=jnp.float32)
                 conv = (
                     pltpu.roll(taps[:, :width], 1, 0)
@@ -365,7 +370,7 @@
         for l in range(leads):
             for j in range(step):
                 at = (l * step + j) * width
-                own = mod_ref[l, j + 1].astype(jnp.float32)
+                own = mod_ref[l, base + j + 1].astype(jnp.float32)
                 out_ref[l, base + j] = (own + mixed[:, at : at + width]).astype(out_ref.dtype)
         return carry
 
@@ -390,7 +395,7 @@
         out_specs=vmem,
         scratch_shapes=[
             pltpu.VMEM((halo_rows, cols, width), jnp.bfloat16),
-            pltpu.VMEM((leads, HEAD_ROWS + 2, cols, width), jnp.bfloat16),
+            pltpu.VMEM((leads, halo_rows, cols, width), jnp.bfloat16),
             pltpu.VMEM((cols, leads * HEAD_ROWS * width), jnp.bfloat16),
             pltpu.VMEM((3 * width, 3 * width), jnp.bfloat16),
             pltpu.SemaphoreType.DMA((pieces * 7,)),
@@ -398,7 +403,7 @@
             pltpu.SemaphoreType.DMA((pieces,)),
         ],
         compiler_params=pltpu.CompilerParams(
-            collective_id=0, has_side_effects=True, vmem_limit_bytes=56 * 1024 * 1024
+            collective_id=0, has_side_effects=True, vmem_limit_bytes=VMEM_ALL
         ),
     )(lead_ids, tile, film_scale, film_shift, w_head, zonal_mix)
 

time: 87.9 us -> 90.2 us (1.026)
  Pallas kernels: 77.4 us -> 78.7 us
  local copies, waits for them, and re-layouts: 10.3 us -> 11.3 us
    pallas_call x1, Pallas kernels: 28.5 us -> 30.4 us  [encoder(): pl.pallas_call(encoder_kernel, out_shape=jax.ShapeDtypeStruct((rows // 2...]
    unnamed x8 -> x2, local copies, waits for them, and re-layouts: 10.3 us -> 11.3 us
where the time goes in v9:
time: 90.2 us; the launch traced here: 90 us
  Pallas kernels  78.7 us (87%)
  local copies, waits for them, and re-layouts  11.3 us (13%)
    pallas_call x1, Pallas kernels, head(): pl.pallas_call(head_kernel, out_shape=jax.ShapeDtypeStruct((leads, rows,...  48.3 us
    pallas_call x1, Pallas kernels, encoder(): pl.pallas_call(encoder_kernel, out_shape=jax.ShapeDtypeStruct((rows // 2...  30.4 us
    unnamed x2, local copies, waits for them, and re-layouts  11.3 us

profile of v9, /device:TPU:24, one launch (start us, length us, event | category | flops | bytes accessed | tf_op | source)
XLA Modules:
  0.0 90.0 jit_solution(16754571280943437025)
XLA Ops:
  0.0 4.7 %copy.9.x_hbm = bf16[40,180,256]{2,1,0:T(8,128)(2,1)} copy(bf16[40,180,256]{2,0,1:T(8,128)(2,1)} %param.8) | data formatting | bytes 7372800 | tf_op args[0]
  4.7 30.4 %shard_map.82.tile_ref = bf16[22,90,128]{2,1,0:T(8,128)(2,1)} custom-call(bf16[40,180,256]{2,1,0:T(8,128)(2,1)} %copy.9.x_hbm, bf16[3,3,256,256]{3,2,1,0:T(8,128)(2,1)} %w_in.2, bf16[256,128]{1,0:T(8,128)(2,1)} %proj_ref.1), custom_call_target="tpu_custom_call" | custom-call | tf_op jit(solution)/shard_map/pallas_call | solution.py:206
  35.1 48.3 %shard_map.83 = bf16[2,20,720,128]{3,2,1,0:T(8,128)(2,1)} custom-call(s32[16]{0:T(128)} %ids_ref.1, bf16[22,90,128]{2,1,0:T(8,128)(2,1)} %shard_map.82.tile_ref, f32[720,128]{1,0:T(8,128)} %scale_ref.1, f32[720,128]{1,0:T(8,128)} %shift_ref.1, bf16[3,3,128,128]{3,2,1,0:T(8,128)(2,1)} %w_in.3, bf16[720,720]{1,0:T(8,128)(2,1)} %mix_ref.1), custom_call_target="tpu_custom_call" | custom-call | tf_op jit(solution)/shard_map/pallas_call | solution.py:391
  83.3 6.6 %copy.11 = bf16[2,20,720,128]{3,2,1,0:T(8,128)(2,1)} copy(bf16[2,20,720,128]{3,2,1,0:T(8,128)(2,1)} %shard_map.83) | data formatting | bytes 14745600
